TPU v7x, 128 devices: a whole 4x4x4 slice. The times are simulated.
128 devices in a mesh: fsdp: 4 (over y_lo, core), expert: 32 (over z, y_hi, x).
Axes of the slice: x: 4, y: 4 (y_hi: 2, y_lo: 2; y = y_hi * 2 + y_lo), z: 4, core: 2. Of those that a mesh axis runs over, the one named last changes fastest.
Arguments:
- tokens: bfloat16 [3, 512, 7168], P(None, 'expert'), may hold values from -6 to 6
- route_ids: int32 [3, 512, 8], P(None, 'expert'), may hold values from 0 to 31, all different within a row; in each aligned block of 16 rows (0 to 15, 16 to 31, ..., all dimensions but the last counted through in order) at most 6 rows name the same one
- gate_values: bfloat16 [3, 512, 8], P(None, 'expert'), may hold values from 0.25 to 1
- cap_limit: int32 [32], replicated, may hold values from 3 to 6
- update_ids: int32 [32], replicated, may hold values from 0 to 31, each once
- expert_weights: bfloat16 [32, 7168, 3072], P(None, ('fsdp', 'expert')), may hold values from -0.109375 to 0.109375
Outputs:
- moe_output: bfloat16 [3, 512, 7168], P(None, 'expert', 'fsdp')
Inputs may be any that keep to these rules, and one draw needn't show every extreme that they name: `route_ids`: each row names 8 different experts. In every aligned block of 16 rows of one step (the rows of one device) no expert is named by more than 6 rows, a bound that some block reaches. `update_ids`: each expert once.
All inputs are finite; a program needn't handle non-finite values.
Results may differ from a plain program's by a relative error of at most 0.0058.
Values may be sent and summed in bfloat16 or wider, within the bound.
No kernel may reach another device: no remote copies, remote signals or barrier semaphores. Data moves between devices by JAX's collectives and lax.ppermute only.
A program may use at most 128 MiB of HBM per device.

v0:
```python
import jax
import jax.numpy as jnp
from jax import lax
from jax.sharding import PartitionSpec as P


def slot_tables(route_block, gate_block, cap_limit, slot_count):
    row_count, top_count = route_block.shape
    experts = cap_limit.shape[0]
    flat_ids = route_block.reshape(row_count * top_count)
    expert_hot = (flat_ids[:, None] == jnp.arange(experts, dtype=jnp.int32)[None, :]).astype(
        jnp.int32
    )
    running = jnp.cumsum(expert_hot, axis=0) - 1
    position = jnp.sum(running * expert_hot, axis=1)
    limit_row = jnp.sum(expert_hot * cap_limit[None, :], axis=1)
    kept_mask = position < limit_row
    slot_index = flat_ids * slot_count + position
    slot_match = slot_index[:, None] == jnp.arange(experts * slot_count, dtype=jnp.int32)[None, :]
    slot_hot = jnp.where(kept_mask[:, None], slot_match, False).astype(jnp.bfloat16)
    row_match = (
        jnp.arange(row_count * top_count, dtype=jnp.int32)[:, None] // top_count
        == jnp.arange(row_count, dtype=jnp.int32)[None, :]
    )
    row_hot = row_match.astype(jnp.bfloat16)
    dispatch_mat = lax.dot_general(
        slot_hot, row_hot, (((0,), (0,)), ((), ())), preferred_element_type=jnp.float32
    ).astype(jnp.bfloat16)
    weighted = slot_hot * gate_block.reshape(row_count * top_count)[:, None]
    combine_mat = lax.dot_general(
        row_hot, weighted, (((0,), (0,)), ((), ())), preferred_element_type=jnp.float32
    ).astype(jnp.bfloat16)
    return (dispatch_mat, combine_mat)


def body(tokens, route_ids, gate_values, cap_limit, update_ids, expert_weights):
    step_count, row_count, model_width = tokens.shape
    top_count = route_ids.shape[2]
    experts = cap_limit.shape[0]
    fsdp_count = lax.axis_size("fsdp")
    slot_count = min(row_count, 3 * row_count * top_count // (2 * experts))
    local_rows = expert_weights.shape[1]
    hidden_all = expert_weights.shape[2] // 3
    hidden_share = hidden_all // fsdp_count
    inverse_order = jnp.argsort(update_ids)
    ordered = jnp.take(expert_weights, inverse_order, axis=0)
    pieces = ordered.reshape(experts, local_rows, 3, fsdp_count, hidden_share)
    pieces = jnp.transpose(pieces, (3, 0, 1, 2, 4))
    outgoing = pieces.reshape(fsdp_count * experts, local_rows, 3 * hidden_share)
    arrived = lax.all_to_all(outgoing, ("fsdp", "expert"), split_axis=0, concat_axis=0, tiled=True)
    owned_block = arrived.reshape(model_width, 3, hidden_share)
    gate_w = owned_block[:, 0, :]
    up_w = owned_block[:, 1, :]
    down_t = owned_block[:, 2, :]
    results = []
    for step_index in range(step_count):
        dispatch_mat, combine_mat = slot_tables(
            route_ids[step_index], gate_values[step_index], cap_limit, slot_count
        )
        sending = jnp.dot(
            dispatch_mat, tokens[step_index], preferred_element_type=jnp.float32
        ).astype(jnp.bfloat16)
        sending = sending.reshape(experts, slot_count, model_width)
        received = lax.all_to_all(sending, "expert", split_axis=0, concat_axis=0, tiled=True)
        item_count = received.shape[1]
        flat_rows = received.reshape(-1, model_width)
        gate_part = jnp.dot(flat_rows, gate_w, preferred_element_type=jnp.float32)
        up_part = jnp.dot(flat_rows, up_w, preferred_element_type=jnp.float32)
        hidden = (jax.nn.silu(gate_part) * up_part).astype(jnp.bfloat16)
        partial_out = lax.dot_general(
            hidden, down_t, (((1,), (1,)), ((), ())), preferred_element_type=jnp.float32
        )
        partial_out = partial_out.reshape(received.shape[0], item_count, model_width)
        reduced = lax.psum_scatter(partial_out, "fsdp", scatter_dimension=2, tiled=True).astype(
            jnp.bfloat16
        )
        returned = lax.all_to_all(reduced, "expert", split_axis=0, concat_axis=0, tiled=True)
        mixed_rows = jnp.dot(
            combine_mat,
            returned.reshape(experts * slot_count, -1),
            preferred_element_type=jnp.float32,
        )
        results.append(mixed_rows.astype(jnp.bfloat16))
    return jnp.stack(results)


def solution(mesh):
    return jax.shard_map(
        body,
        mesh=mesh,
        in_specs=(
            P(None, "expert", None),
            P(None, "expert", None),
            P(None, "expert", None),
            P(),
            P(),
            P(None, ("fsdp", "expert"), None),
        ),
        out_specs=P(None, "expert", "fsdp"),
        check_vma=False,
    )
```

profile of v0, /device:TPU:0, one launch (start us, length us, event | category | flops | bytes accessed | tf_op | source)
XLA Modules:
  0.0 628.9 jit_solution(6357448450625726888)
XLA Ops:
  6.5 0.7 fusion.152
  8.6 0.9 select_reduce_fusion.4
  9.5 2.1 convolution_convert_fusion.2
  11.6 2.7 reshape.129
  14.3 11.1 %all-to-all-start = ((bf16[32,6,7168]{2,1,0:T(8,128)(2,1)}), bf16[32,6,7168]{2,1,0:T(8,128)(2,1)}, u32[]{:S(2)}, u32[]{:S(2)}) async-start(bf16[32,6,7168]{2,1,0:T(8,128)(2,1)} %reshape.129), calls=%async_computation | async-start | bytes 7340032 | tf_op jit(solution)/shard_map/all_to_all | solution.py:64
  25.5 1.6 sort.17
  27.1 10.4 %gather_fusion = bf16[32,56,3072]{2,1,0:T(8,128)(2,1)} fusion(bf16[32,56,3072]{2,1,0:T(8,128)(2,1)} %param.11, s32[1024]{0:T(1024)S(1)} %pad_clamp_fusion), kind=kCustom, calls=%fused_computation | custom fusion | bytes 22020224 | tf_op jit(solution)/shard_map/jit(_take)/gather | solution.py:46
  37.5 20.5 %gather.7 = bf16[32,56,3,4,256]{4,3,2,1,0:T(4,128)(2,1)} reshape(bf16[32,56,3072]{2,1,0:T(8,128)(2,1)} %gather_fusion) | data formatting | bytes 22020096 | tf_op jit(solution)/shard_map/jit(_take)/gather | solution.py:46
  58.0 18.0 %fusion = bf16[4,32,56,3,256]{4,3,2,1,0:T(4,128)(2,1)} fusion(bf16[32,56,3,4,256]{4,3,2,1,0:T(4,128)(2,1)} %gather.7, pred[32]{0:T(512)(128)(4,1)S(1)} %compare_and_fusion), kind=kLoop, calls=%fused_computation.2 | loop fusion | flops 5505024 | bytes 22020128 | tf_op jit(solution)/shard_map/transpose | solution.py:48
  76.1 29.5 %reshape.131 = bf16[128,56,768]{2,1,0:T(8,128)(2,1)} reshape(bf16[4,32,56,3,256]{4,3,2,1,0:T(4,128)(2,1)} %fusion) | data formatting | bytes 22020096 | tf_op jit(solution)/shard_map/reshape | solution.py:49
  105.6 10.5 %all-to-all-start.1 = ((bf16[128,56,768]{2,1,0:T(8,128)(2,1)}), bf16[128,56,768]{2,1,0:T(8,128)(2,1)}, u32[]{:S(2)}, u32[]{:S(2)}) async-start(bf16[128,56,768]{2,1,0:T(8,128)(2,1)} %reshape.131), calls=%async_computation.1 | async-start | bytes 22020096 | tf_op jit(solution)/shard_map/all_to_all | solution.py:50
  116.3 3.2 reshape.130
  119.5 138.1 %all-to-all-done.1 = bf16[128,56,768]{2,1,0:T(8,128)(2,1)} async-done(((bf16[128,56,768]{2,1,0:T(8,128)(2,1)}), bf16[128,56,768]{2,1,0:T(8,128)(2,1)}, u32[]{:S(2)}, u32[]{:S(2)}) %all-to-all-start.1) | async-done | bytes 11010080 | tf_op jit(solution)/shard_map/all_to_all | solution.py:50
  257.6 29.3 %reshape.132 = bf16[7168,3,256]{2,1,0:T(4,128)(2,1)} reshape(bf16[128,56,768]{2,1,0:T(8,128)(2,1)} %all-to-all-done.1) | data formatting | bytes 22020096 | tf_op jit(solution)/shard_map/reshape | solution.py:51
  286.9 27.1 %fusion.151 = (bf16[7168,1,256]{2,1,0:T(2,128)(2,1)}, bf16[7168,1,256]{2,1,0:T(2,128)(2,1)}, bf16[7168,1,256]{2,1,0:T(2,128)(2,1)}) fusion(bf16[7168,3,256]{2,1,0:T(4,128)(2,1)} %reshape.132), kind=kLoop, calls=%fused_computation.127 | loop fusion | bytes 22020096 | tf_op jit(solution)/shard_map/slice | solution.py:54
  314.0 4.1 fusion.11
  318.1 1.0 copy-done
  319.2 1.0 fusion.31
  320.2 6.8 %fusion.56 = f32[32,6,7168]{2,0,1:T(8,128)} fusion(bf16[32,6,256]{2,1,0:T(8,128)(2,1)S(1)} %dot_general.74, bf16[7168,1,256]{2,1,0:T(2,128)(2,1)} %get-tuple-element.13), kind=kOutput, calls=%fused_computation.57 | convolution fusion | flops 704643072 | bytes 9273344 | tf_op jit(solution)/shard_map/dot_general | solution.py:70
  327.1 2.1 convolution_convert_fusion.1
  329.2 2.7 reshape.134
  331.9 63.1 %all_to_all.35 = bf16[32,6,7168]{2,1,0:T(8,128)(2,1)} all-to-all(bf16[32,6,7168]{2,1,0:T(8,128)(2,1)} %reshape.134), channel_id=1, replica_groups=mesh['fsdp'=4,'expert'=32] {'expert'}, dimensions={0} | all-to-all | bytes 5505024 | tf_op jit(solution)/shard_map/all_to_all | solution.py:64
  395.0 4.8 reshape.135
  399.9 5.1 fusion.9
  405.1 0.9 copy-done.2
  406.0 1.0 fusion.28
  407.0 6.9 %fusion.54 = f32[32,6,7168]{2,0,1:T(8,128)} fusion(bf16[32,6,256]{2,1,0:T(8,128)(2,1)S(1)} %dot_general.82, bf16[7168,1,256]{2,1,0:T(2,128)(2,1)} %get-tuple-element.13), kind=kOutput, calls=%fused_computation.55 | convolution fusion | flops 704643072 | bytes 9273344 | tf_op jit(solution)/shard_map/dot_general | solution.py:70
  414.0 2.1 convolution_convert_fusion
  416.1 2.7 reshape.137
  418.8 56.5 %all_to_all.36 = bf16[32,6,7168]{2,1,0:T(8,128)(2,1)} all-to-all(bf16[32,6,7168]{2,1,0:T(8,128)(2,1)} %reshape.137), channel_id=1, replica_groups=mesh['fsdp'=4,'expert'=32] {'expert'}, dimensions={0} | all-to-all | bytes 5505024 | tf_op jit(solution)/shard_map/all_to_all | solution.py:64
  475.3 4.8 reshape.138
  480.1 5.0 fusion.7
  485.3 0.9 copy-done.1
  486.2 1.0 fusion.25
  487.2 6.9 %fusion.52 = f32[32,6,7168]{2,0,1:T(8,128)} fusion(bf16[32,6,256]{2,1,0:T(8,128)(2,1)S(1)} %dot_general.90, bf16[7168,1,256]{2,1,0:T(2,128)(2,1)} %get-tuple-element.13), kind=kOutput, calls=%fused_computation.53 | convolution fusion | flops 704643072 | bytes 9273344 | tf_op jit(solution)/shard_map/dot_general | solution.py:70
  494.2 1.5 convert_element_type.74
  495.7 1.3 copy.49
  497.0 7.0 %all-to-all-start.2 = ((bf16[32,6,1792]{2,1,0:T(8,128)(2,1)}), bf16[32,6,1792]{2,1,0:T(8,128)(2,1)S(1)}, u32[]{:S(2)}, u32[]{:S(2)}) async-start(bf16[32,6,1792]{2,1,0:T(8,128)(2,1)} %copy.49), calls=%async_computation.3 | async-start | bytes 1835008 | tf_op jit(solution)/shard_map/all_to_all | solution.py:77
  504.0 19.0 %reduce-scatter.6.cloned.1.call-done = f32[32,6,1792]{2,0,1:T(8,128)} async-done(((f32[32,6,7168]{2,0,1:T(8,128)}), f32[32,6,1792]{2,0,1:T(8,128)}) %reduce-scatter.6.cloned.1.call-update) | async-done | bytes 1376272 | tf_op jit(solution)/shard_map/reduce_scatter | solution.py:74
  523.0 1.4 convert_element_type.81
  524.4 1.4 copy.53
  525.8 10.0 %all-to-all-start.4 = ((bf16[32,6,1792]{2,1,0:T(8,128)(2,1)}), bf16[32,6,1792]{2,1,0:T(8,128)(2,1)S(1)}, u32[]{:S(2)}, u32[]{:S(2)}) async-start(bf16[32,6,1792]{2,1,0:T(8,128)(2,1)} %copy.53), calls=%async_computation.6 | async-start | bytes 1835008 | tf_op jit(solution)/shard_map/all_to_all | solution.py:77
  535.8 55.4 %reduce-scatter.8.cloned.1.call-done = f32[32,6,1792]{2,0,1:T(8,128)} async-done(((f32[32,6,7168]{2,0,1:T(8,128)}), f32[32,6,1792]{2,0,1:T(8,128)}) %reduce-scatter.8.cloned.1.call-update) | async-done | bytes 1376272 | tf_op jit(solution)/shard_map/reduce_scatter | solution.py:74
  591.2 1.4 convert_element_type.88
  592.6 1.3 copy.57
  593.9 10.2 %all-to-all-start.6 = ((bf16[32,6,1792]{2,1,0:T(8,128)(2,1)}), bf16[32,6,1792]{2,1,0:T(8,128)(2,1)S(1)}, u32[]{:S(2)}, u32[]{:S(2)}) async-start(bf16[32,6,1792]{2,1,0:T(8,128)(2,1)} %copy.57), calls=%async_computation.9 | async-start | bytes 1835008 | tf_op jit(solution)/shard_map/all_to_all | solution.py:77
  606.1 14.9 %all-to-all-done.6 = bf16[32,6,1792]{2,1,0:T(8,128)(2,1)S(1)} async-done(((bf16[32,6,1792]{2,1,0:T(8,128)(2,1)}), bf16[32,6,1792]{2,1,0:T(8,128)(2,1)S(1)}, u32[]{:S(2)}, u32[]{:S(2)}) %all-to-all-start.6) | async-done | bytes 688160 | tf_op jit(solution)/shard_map/all_to_all | solution.py:77
  621.6 0.7 pad_maximum_fusion
  (66 shorter events, 4.8 us)
Async XLA Ops:
  14.3 11.2 %copy-start.4 = (s32[32]{0:T(128)S(1)}, s32[32]{0:T(128)}, u32[]{:S(2)}) copy-start(s32[32]{0:T(128)} %param.10) | copy-start | bytes 388
  14.3 91.3 %all-to-all-start = ((bf16[32,6,7168]{2,1,0:T(8,128)(2,1)}), bf16[32,6,7168]{2,1,0:T(8,128)(2,1)}, u32[]{:S(2)}, u32[]{:S(2)}) async-start(bf16[32,6,7168]{2,1,0:T(8,128)(2,1)} %reshape.129), calls=%async_computation | async-start | bytes 7340032 | tf_op jit(solution)/shard_map/all_to_all | solution.py:64
  105.6 152.0 %all-to-all-start.1 = ((bf16[128,56,768]{2,1,0:T(8,128)(2,1)}), bf16[128,56,768]{2,1,0:T(8,128)(2,1)}, u32[]{:S(2)}, u32[]{:S(2)}) async-start(bf16[128,56,768]{2,1,0:T(8,128)(2,1)} %reshape.131), calls=%async_computation.1 | async-start | bytes 22020096 | tf_op jit(solution)/shard_map/all_to_all | solution.py:50
  116.1 378.1 %reduce-scatter.4.cloned.1.call-start = ((), (), s32[]{:S(2)}) async-start(), calls=%async_computation.10 | async-start | bytes 6881280 | tf_op jit(solution)/shard_map/reduce_scatter | solution.py:74
  314.0 5.2 copy-start
  327.1 196.0 %reduce-scatter.6.cloned.1.call-start = ((), (), s32[]{:S(2)}) async-start(), calls=%async_computation.11 | async-start | bytes 6881280 | tf_op jit(solution)/shard_map/reduce_scatter | solution.py:74
  395.0 9.9 %slice-start = ((s8[7340032]{0:T(1024)(128)(4,1)}), s8[3145728]{0:T(1024)(128)(4,1)S(1)}, s32[]{:S(2)}) async-start(s8[7340032]{0:T(1024)(128)(4,1)} %bitcast.58), calls=%async_computation.13 | async-start | bytes 6291456
  399.9 5.2 slice-start.1
  399.9 6.1 copy-start.2
  413.9 177.3 %reduce-scatter.8.cloned.1.call-start = ((), (), s32[]{:S(2)}) async-start(), calls=%async_computation.12 | async-start | bytes 6881280 | tf_op jit(solution)/shard_map/reduce_scatter | solution.py:74
  475.3 9.8 %slice-start.2 = ((s8[7340032]{0:T(1024)(128)(4,1)}), s8[3145728]{0:T(1024)(128)(4,1)S(1)}, s32[]{:S(2)}) async-start(s8[7340032]{0:T(1024)(128)(4,1)} %bitcast.60), calls=%async_computation.15 | async-start | bytes 6291456
  480.1 5.2 slice-start.3
  480.1 6.1 copy-start.1
  497.0 28.8 %all-to-all-start.2 = ((bf16[32,6,1792]{2,1,0:T(8,128)(2,1)}), bf16[32,6,1792]{2,1,0:T(8,128)(2,1)S(1)}, u32[]{:S(2)}, u32[]{:S(2)}) async-start(bf16[32,6,1792]{2,1,0:T(8,128)(2,1)} %copy.49), calls=%async_computation.3 | async-start | bytes 1835008 | tf_op jit(solution)/shard_map/all_to_all | solution.py:77
  525.8 78.3 %copy-start.3 = (bf16[3,16,8]{1,2,0:T(8,128)(2,1)S(1)}, bf16[3,16,8]{1,2,0:T(8,128)(2,1)}, u32[]{:S(2)}) copy-start(bf16[3,16,8]{1,2,0:T(8,128)(2,1)} %param.8) | copy-start | bytes 2308
  525.8 68.1 %all-to-all-start.4 = ((bf16[32,6,1792]{2,1,0:T(8,128)(2,1)}), bf16[32,6,1792]{2,1,0:T(8,128)(2,1)S(1)}, u32[]{:S(2)}, u32[]{:S(2)}) async-start(bf16[32,6,1792]{2,1,0:T(8,128)(2,1)} %copy.53), calls=%async_computation.6 | async-start | bytes 1835008 | tf_op jit(solution)/shard_map/all_to_all | solution.py:77
  593.9 27.0 %all-to-all-start.6 = ((bf16[32,6,1792]{2,1,0:T(8,128)(2,1)}), bf16[32,6,1792]{2,1,0:T(8,128)(2,1)S(1)}, u32[]{:S(2)}, u32[]{:S(2)}) async-start(bf16[32,6,1792]{2,1,0:T(8,128)(2,1)} %copy.57), calls=%async_computation.9 | async-start | bytes 1835008 | tf_op jit(solution)/shard_map/all_to_all | solution.py:77
Sparse Core Ops, SparseCore 0:
  327.2 96.2 reduce-scatter.3
  425.9 97.0 reduce-scatter.5
  525.4 65.7 reduce-scatter.7
where the time goes:
time: 632 us; the launch traced here: 629 us
  waiting for transfers between devices  227 us (36%)
  local copies, waits for them, and re-layouts  148 us (23%)
  blocking collectives  120 us (19%)
  starting transfers between devices  49.2 us (8%)
  matrix products  45.4 us (7%)
  other arithmetic  26.4 us (4%)
  between operations  13.5 us (2%)
    all_to_all x1, waiting for transfers between devices, body(): lax.all_to_all(outgoing, ('fsdp', 'expert'), split_axis=0, concat_axis=0,...  138 us
    all_to_all x2, blocking collectives, body(): lax.all_to_all(sending, 'expert', split_axis=0, concat_axis=0, tiled=True)  120 us
    reduce_scatter x3, waiting for transfers between devices, body(): lax.psum_scatter(partial_out, 'fsdp', scatter_dimension=2, tiled=True)  74.4 us
    gather x2, local copies, waits for them, and re-layouts, body(): ordered = jnp.take(expert_weights, inverse_order, axis=0)  30.9 us
    reshape x1, local copies, waits for them, and re-layouts, body(): pieces.reshape(fsdp_count * experts, local_rows, 3 * hidden_share)  29.5 us
    reshape x1, local copies, waits for them, and re-layouts, body(): owned_block = arrived.reshape(model_width, 3, hidden_share)  29.3 us
    all_to_all x3, starting transfers between devices, body(): lax.all_to_all(reduced, 'expert', split_axis=0, concat_axis=0, tiled=True)  27.2 us
    slice x1, local copies, waits for them, and re-layouts, body(): down_t = owned_block[:, 2, :]  27.1 us
  transfers between devices with their start and end apart: 8, of which 4 were waited for; matrix products, arithmetic and copies ran while one was open for 22% of the time, Pallas kernels for 0%

commit v1 on v0

v1 whole, which is shorter than its diff:
```python
import jax
import jax.numpy as jnp
from jax import lax
from jax.experimental import pallas as pl
from jax.experimental.pallas import tpu as pltpu
from jax.sharding import PartitionSpec as P


CORE_SWAP = ((0, 1), (1, 0), (2, 3), (3, 2))
CHIP_SWAP = ((0, 2), (2, 0), (1, 3), (3, 1))


def routing(route_ids, gate_values, cap_limit, update_ids, slot_count):
    steps, rows, top = route_ids.shape
    experts = cap_limit.shape[0]
    choices = steps * rows * top
    flat_ids = route_ids.reshape(choices)
    hot = (flat_ids[:, None] == jnp.arange(experts, dtype=jnp.int32)[None, :]).astype(jnp.bfloat16)
    number = jnp.arange(choices, dtype=jnp.int32)
    per_step = rows * top
    earlier = (number[:, None] > number[None, :]) & (
        number[:, None] // per_step == number[None, :] // per_step
    )
    before = jnp.dot(earlier.astype(jnp.bfloat16), hot, preferred_element_type=jnp.float32)
    hot32 = hot.astype(jnp.float32)
    position = jnp.sum(before * hot32, axis=1).astype(jnp.int32)
    limit = jnp.sum(hot32 * cap_limit.astype(jnp.float32)[None, :], axis=1).astype(jnp.int32)
    holder = jnp.sum(
        jnp.where(
            update_ids[:, None] == jnp.arange(experts, dtype=jnp.int32)[None, :],
            jnp.arange(experts, dtype=jnp.int32)[:, None],
            0,
        ),
        axis=0,
    )
    owner = jnp.sum(hot32 * holder.astype(jnp.float32)[None, :], axis=1).astype(jnp.int32)
    count = steps * slot_count
    first = 16
    within = (number // per_step) * slot_count + position
    slot = jnp.where(
        within < first,
        owner * first + within,
        experts * first + owner * (count - first) + within - first,
    )
    slot = jnp.where(position < limit, slot, -1).reshape(steps * rows, top)
    total = experts * count
    at = jnp.arange(total, dtype=jnp.int32)
    gates = gate_values.reshape(steps * rows, top).astype(jnp.float32)
    dispatch = jnp.zeros((total, steps * rows), jnp.float32)
    combine = jnp.zeros((steps * rows, total), jnp.float32)
    for k in range(top):
        dispatch = dispatch + (at[:, None] == slot[:, k][None, :]).astype(jnp.float32)
        combine = combine + jnp.where(at[None, :] == slot[:, k][:, None], gates[:, k][:, None], 0.0)
    return dispatch.astype(jnp.bfloat16), combine.astype(jnp.bfloat16)


def exchange(block):
    return lax.all_to_all(block, "expert", split_axis=0, concat_axis=0, tiled=True)


def pack_kernel(weights_ref, beside_ref, first_ref, second_ref):
    wide = weights_ref.shape[2] // 3 * 2
    first_ref[:, :, :wide] = weights_ref[:, :, :wide]
    first_ref[:, :, wide:] = beside_ref[...]
    second_ref[...] = weights_ref[:, :, wide:]


def pack(weights, beside):
    experts, local, columns = weights.shape
    hidden = columns // 3
    extra = beside.shape[2]
    batch = 4
    block = lambda width: pl.BlockSpec((batch, local, width), lambda i: (i, 0, 0))
    return pl.pallas_call(
        pack_kernel,
        grid=(experts // batch,),
        in_specs=[block(columns), block(extra)],
        out_specs=[block(2 * hidden + extra), block(hidden)],
        out_shape=[
            jax.ShapeDtypeStruct((experts, local, 2 * hidden + extra), weights.dtype),
            jax.ShapeDtypeStruct((experts, local, hidden), weights.dtype),
        ],
        name="pack",
    )(weights, beside)


def gate_up_kernel(core_ref, arrived_ref, passed_ref, kept_ref, weights, rows, tail, sems):
    experts, local, _ = arrived_ref.shape
    quarter = weights.shape[3]
    wide = 4 * quarter
    share = rows.shape[2]
    main = experts * 16
    core = core_ref[0]
    copies = [
        pltpu.make_async_copy(
            arrived_ref.at[:, pl.ds(16 * b, 16), pl.ds(wide, w)],
            rows.at[:, :, pl.ds(640 * b, w)],
            sems.at[b],
        )
        for b, w in enumerate((640, 640, share - 1280))
    ]
    copies.append(
        pltpu.make_async_copy(arrived_ref.at[:, pl.ds(48, 8), pl.ds(wide, 512)], tail, sems.at[3])
    )
    starts = [(1 - core) * quarter, (1 - core) * quarter + 2 * quarter]
    starts += [core * quarter, core * quarter + 2 * quarter]
    for i, start in enumerate(starts):
        copies.append(
            pltpu.make_async_copy(
                arrived_ref.at[:, :, pl.ds(pl.multiple_of(start, quarter), quarter)],
                weights.at[i],
                sems.at[4 + i],
            )
        )
    for copy in copies:
        copy.start()
    for copy in copies[:4]:
        copy.wait()
    top = rows[...].reshape(main, share)
    flat = tail[...].reshape(experts * 8, 512)
    at = lax.broadcasted_iota(jnp.int32, (2 * experts, 8 * experts), 0)
    of = lax.broadcasted_iota(jnp.int32, (2 * experts, 8 * experts), 1)
    pieces = []
    for q in range(4):
        pick = (of == at * 4 + q).astype(jnp.bfloat16)
        pieces.append(jnp.dot(pick, flat, preferred_element_type=jnp.float32).astype(jnp.bfloat16))
    last = jnp.concatenate(pieces, axis=1)[:, :share]
    for i in range(4):
        copies[4 + i].wait()
        block = weights[i].reshape(experts * local, quarter)
        out_ref = passed_ref if i < 2 else kept_ref
        columns = pl.ds((i % 2) * quarter, quarter)
        out_ref[:main, columns] = jnp.dot(top, block, preferred_element_type=jnp.float32)
        out_ref[main:, columns] = jnp.dot(last, block, preferred_element_type=jnp.float32)


def gate_up(core, arrived, hidden, share):
    experts, local, _ = arrived.shape
    slots = experts * 18
    quarter = hidden // 2
    out = jax.ShapeDtypeStruct((slots, hidden), jnp.float32)
    return pl.pallas_call(
        gate_up_kernel,
        in_specs=[
            pl.BlockSpec(memory_space=pltpu.SMEM),
            pl.BlockSpec(memory_space=pl.ANY),
        ],
        out_specs=[pl.BlockSpec(memory_space=pltpu.VMEM)] * 2,
        out_shape=[out, out],
        scratch_shapes=[
            pltpu.VMEM((4, experts, local, quarter), jnp.bfloat16),
            pltpu.VMEM((experts, 16, share), jnp.bfloat16),
            pltpu.VMEM((experts, 8, 512), jnp.bfloat16),
            pltpu.SemaphoreType.DMA((8,)),
        ],
        compiler_params=pltpu.CompilerParams(vmem_limit_bytes=40 << 20),
        cost_estimate=pl.CostEstimate(
            flops=2 * slots * share * 2 * hidden,
            bytes_accessed=2 * arrived.size + 8 * slots * hidden,
            transcendentals=0,
        ),
        name="gate_up",
    )(core, arrived)


def layer(tokens, route_ids, gate_values, cap_limit, update_ids, expert_weights):
    steps, rows, width = tokens.shape
    experts, _, _ = expert_weights.shape
    fsdp_count = lax.axis_size("fsdp")
    fsdp_at = lax.axis_index("fsdp")
    slot_count = 6
    hidden = expert_weights.shape[2] // 3
    half = hidden // 2
    quarter = half // 2
    share = width // fsdp_count
    main = experts * 16

    dispatch, combine = routing(route_ids, gate_values, cap_limit, update_ids, slot_count)
    own_columns = lax.dynamic_slice_in_dim(
        tokens.reshape(steps * rows, width), fsdp_at * share, share, axis=1
    )
    sending = jnp.dot(dispatch, own_columns, preferred_element_type=jnp.float32).astype(jnp.bfloat16)
    head = sending[:main].reshape(experts, 16, share)
    head = jnp.pad(head, ((0, 0), (0, 0), (0, 1920 - share)))
    tail = jnp.pad(sending[main:], ((0, 0), (0, 2048 - share))).reshape(experts, 8, 512)
    tail = jnp.pad(tail, ((0, 0), (0, 0), (0, 128)))
    beside = jnp.concatenate(
        [head[:, :, :640], head[:, :, 640:1280], head[:, :, 1280:], tail], axis=1
    )
    outgoing, down_raw = pack(expert_weights, beside)
    core = (fsdp_at % 2).astype(jnp.int32)
    upper = fsdp_at // 2 == 1
    second = core == 1
    outgoing, down_raw, combine, core, upper, second = lax.optimization_barrier(
        (outgoing, down_raw, combine, core, upper, second)
    )
    arrived = exchange(outgoing)
    arrived, down_raw = lax.optimization_barrier((arrived, down_raw))
    down = exchange(down_raw).reshape(share, hidden)

    passed, kept = gate_up(core.reshape(1), arrived, hidden, share)
    kept = kept + lax.ppermute(passed, "fsdp", CORE_SWAP)
    g0, g1, u0, u1 = (kept[:, i * quarter : (i + 1) * quarter] for i in range(4))
    send = jnp.concatenate([jnp.where(upper, g0, g1), jnp.where(upper, u0, u1)], axis=1)
    gate = jnp.where(upper, g1, g0)
    up = jnp.where(upper, u1, u0)
    across = lax.ppermute(send.astype(jnp.bfloat16), "fsdp", CHIP_SWAP).astype(jnp.float32)
    act = (jax.nn.silu(gate + across[:, :quarter]) * (up + across[:, quarter:])).astype(jnp.bfloat16)
    other = lax.ppermute(act, "fsdp", CHIP_SWAP)
    act = jnp.concatenate([jnp.where(upper, other, act), jnp.where(upper, act, other)], axis=1)
    other = lax.ppermute(act, "fsdp", CORE_SWAP)
    act = jnp.concatenate([jnp.where(second, other, act), jnp.where(second, act, other)], axis=1)
    out = lax.dot_general(
        act, down, (((1,), (1,)), ((), ())), preferred_element_type=jnp.float32
    ).astype(jnp.bfloat16)
    rest = out[main:].reshape(experts, 14, 256)
    rest = jnp.pad(rest, ((0, 0), (0, 2), (0, 0)))
    going = jnp.concatenate([out[:main].reshape(experts, 16, share), rest], axis=2)
    returned = exchange(going)
    mixed = jnp.dot(
        combine[:, :main],
        returned[:, :, :share].reshape(main, share),
        preferred_element_type=jnp.float32,
    ) + jnp.dot(
        combine[:, main:],
        returned[:, :14, share:].reshape(experts * 2, share),
        preferred_element_type=jnp.float32,
    )
    return mixed.astype(jnp.bfloat16).reshape(steps, rows, share)


def solution(mesh):
    return jax.shard_map(
        layer,
        mesh=mesh,
        in_specs=(
            P(None, "expert", None),
            P(None, "expert", None),
            P(None, "expert", None),
            P(),
            P(),
            P(None, ("fsdp", "expert"), None),
        ),
        out_specs=P(None, "expert", "fsdp"),
        check_vma=False,
    )
```

time: 632 us -> 275 us (0.44)
  waiting for transfers between devices: 227 us -> 61.1 us
  local copies, waits for them, and re-layouts: 148 us -> 3.44 us
  blocking collectives: 120 us -> 169 us
  starting transfers between devices: 49.2 us -> 8.34 us
  matrix products: 45.4 us -> 6.77 us
  other arithmetic: 26.4 us -> 6.62 us
  Pallas kernels: 0 us -> 18.4 us
  between operations: 13.5 us -> 0.32 us
    all_to_all x5 -> x1, waiting for transfers between devices: 153 us -> 0.01 us  [exchange(): lax.all_to_all(block, 'expert', split_axis=0, concat_axis=0, tiled=True)]
    reshape x11 -> x3, local copies, waits for them, and re-layouts: 80.6 us -> 0.67 us  [the longest x1 0.25 us: layer(): returned[:, :14, share:].reshape(experts * 2, share)]
    reduce_scatter x3 -> x0, waiting for transfers between devices: 74.4 us -> none  [body(): lax.psum_scatter(partial_out, 'fsdp', scatter_dimension=2, tiled=True)]
    ppermute x0 -> x4, waiting for transfers between devices: none -> 61.1 us  [the longest x1 52 us: layer(): lax.ppermute(send.astype(jnp.bfloat16), 'fsdp', CHIP_SWAP)]
    all_to_all x2, blocking collectives: 120 us -> 169 us  [exchange(): lax.all_to_all(block, 'expert', split_axis=0, concat_axis=0, tiled=True)]
    all_to_all x5 -> x1, starting transfers between devices: 48.9 us -> 4.84 us  [exchange(): lax.all_to_all(block, 'expert', split_axis=0, concat_axis=0, tiled=True)]
    dot_general x15 -> x5, matrix products: 45.4 us -> 6.77 us  [the longest x1 4.37 us: layer(): lax.dot_general(act, down, (((1,), (1,)), ((), ())), preferred_element_ty...]
    gather x2 -> x0, local copies, waits for them, and re-layouts: 30.9 us -> none  [body(): ordered = jnp.take(expert_weights, inverse_order, axis=0)]
  transfers between devices with their start and end apart: 8 -> 5, of which waited for: 4 -> 3; matrix products, arithmetic and copies ran while one was open for 22% -> 1% of each run, Pallas kernels for 0% -> 0%
where the time goes in v1:
time: 275 us; the launch traced here: 274 us
  blocking collectives  169 us (61%)
  waiting for transfers between devices  61.1 us (22%)
  Pallas kernels  18.4 us (7%)
  starting transfers between devices  8.34 us (3%)
  matrix products  6.77 us (2%)
  other arithmetic  6.62 us (2%)
  local copies, waits for them, and re-layouts  3.44 us (1%)
    all_to_all x2, blocking collectives, exchange(): lax.all_to_all(block, 'expert', split_axis=0, concat_axis=0, tiled=True)  169 us
    ppermute x1, waiting for transfers between devices, layer(): lax.ppermute(send.astype(jnp.bfloat16), 'fsdp', CHIP_SWAP)  52 us
    pallas_call x1, Pallas kernels, pack(): pl.pallas_call(pack_kernel, grid=(experts // batch,), in_specs=[block(col...  11.5 us
    ppermute x1, waiting for transfers between devices, layer(): other = lax.ppermute(act, 'fsdp', CHIP_SWAP)  7.08 us
    pallas_call x1, Pallas kernels, gate_up(): pl.pallas_call(gate_up_kernel, in_specs=[pl.BlockSpec(memory_space=pltpu....  6.83 us
  transfers between devices with their start and end apart: 5, of which 3 were waited for; matrix products, arithmetic and copies ran while one was open for 1% of the time, Pallas kernels for 0%

profile of v1, /device:TPU:0, one launch (start us, length us, event | category | flops | bytes accessed | tf_op | source)
XLA Modules:
  0.0 274.0 jit_solution(17905412244911456207)
XLA Ops:
  0.0 0.7 convert_element_type.100
  0.7 0.7 select_reduce_fusion
  1.5 0.8 copy.11
  2.3 0.1 eq.277
  2.4 0.3 fusion.8
  2.7 0.1 fusion.25
  2.8 0.1 mul.59
  2.9 0.1 convert_element_type.102
  3.0 0.1 convert_element_type.99
  3.1 0.1 add.123
  3.2 0.3 slice_reduce_fusion.7
  3.5 0.8 convolution_convert_fusion
  4.3 0.0 copy-start.2
  4.4 0.1 slice.150
  4.5 0.5 copy-done.2
  5.0 0.1 reshape.151
  5.2 0.2 reshape.143
  5.3 0.2 fusion.42
  5.5 1.5 fusion.2.beside_ref
  7.0 11.5 %pack.1 = (bf16[32,56,2688]{2,1,0:T(8,128)(2,1)}, bf16[32,56,1024]{2,1,0:T(8,128)(2,1)}) custom-call(bf16[32,56,3072]{2,1,0:T(8,128)(2,1)} %weights_ref.1, bf16[32,56,640]{2,1,0:T(8,128)(2,1)} %fusion.2.beside_ref), custom_call_target="tpu_custom_call" | custom-call | tf_op jit(solution)/shard_map/pack/pallas_call | solution.py:74
  18.5 0.2 add_convert_fusion.2
  18.7 122.2 %all_to_all.15.arrived_ref = bf16[32,56,2688]{2,1,0:T(8,128)(2,1)S(1)} all-to-all(bf16[32,56,2688]{2,1,0:T(8,128)(2,1)} %get-tuple-element.23), channel_id=1, replica_groups=mesh['fsdp'=4,'expert'=32] {'expert'}, dimensions={0} | all-to-all | bytes 19267584 | tf_op jit(solution)/shard_map/all_to_all | solution.py:58
  140.9 6.8 %gate_up.1 = (f32[576,1024]{1,0:T(8,128)}, f32[576,1024]{1,0:T(8,128)S(1)}) custom-call(s32[1]{0:T(128)} %bitcast.10.core_ref, bf16[32,56,2688]{2,1,0:T(8,128)(2,1)S(1)} %all_to_all.15.arrived_ref), custom_call_target="tpu_custom_call" | custom-call | flops 4227858432 | bytes 14352384 | tf_op jit(solution)/shard_map/gate_up/pallas_call | solution.py:142
  147.7 0.1 collective-permute-start
  147.8 4.8 %all-to-all-start.1 = ((bf16[32,56,1024]{2,1,0:T(8,128)(2,1)}), bf16[32,56,1024]{2,1,0:T(8,128)(2,1)}, u32[]{:S(2)}, u32[]{:S(2)}) async-start(bf16[32,56,1024]{2,1,0:T(8,128)(2,1)} %get-tuple-element.28), calls=%async_computation.1 | async-start | bytes 7340032 | tf_op jit(solution)/shard_map/all_to_all | solution.py:58
  152.6 0.0 collective-permute-done
  152.7 2.1 add.141
  154.8 0.1 select_convert_fusion.1
  154.9 0.8 collective-permute-start.1
  155.7 52.0 %collective-permute-done.1 = bf16[576,512]{1,0:T(8,128)(2,1)S(1)} collective-permute-done((bf16[576,512]{1,0:T(8,128)(2,1)S(1)}, bf16[576,512]{1,0:T(8,128)(2,1)S(1)}, u32[]{:S(2)}, u32[]{:S(2)}) %collective-permute-start.1) | collective-permute-done | bytes 589856 | tf_op jit(solution)/shard_map/ppermute | solution.py:207
  207.7 0.1 convert_element_type.118
  207.9 0.4 fusion.10
  208.2 2.6 collective-permute-start.2
  210.8 7.1 %collective-permute-done.2 = bf16[576,256]{1,0:T(8,128)(2,1)S(1)} collective-permute-done((bf16[576,256]{1,0:T(8,128)(2,1)S(1)}, bf16[576,256]{1,0:T(8,128)(2,1)S(1)}, u32[]{:S(2)}, u32[]{:S(2)}) %collective-permute-start.2) | collective-permute-done | bytes 294944 | tf_op jit(solution)/shard_map/ppermute | solution.py:209
  218.0 0.1 collective-permute-start.3
  218.1 2.0 collective-permute-done.3
  220.1 0.2 broadcast_select_fusion.1
  220.3 0.0 all-to-all-done.1
  220.3 4.4 %convolution_convert_fusion.1 = bf16[576,1792]{1,0:T(8,128)(2,1)S(1)} fusion(bf16[1792,1024]{1,0:T(8,128)(2,1)} %bitcast.11, bf16[576,512]{1,0:T(8,128)(2,1)S(1)} %get-tuple-element.45, bf16[576,512]{1,0:T(8,128)(2,1)S(1)} %get-tuple-element.44), kind=kOutput, calls=%fused_computation.5 | convolution fusion | flops 2117320704 | bytes 6914048 | tf_op jit(solution)/shard_map/dot_general | solution.py:213
  224.7 0.1 slice.160
  224.8 0.3 reshape.147
  225.1 0.3 fusion.4
  225.4 46.8 %all_to_all.16 = bf16[32,16,2048]{2,1,0:T(8,128)(2,1)S(1)} all-to-all(bf16[32,16,2048]{2,1,0:T(8,128)(2,1)S(1)} %fusion.4), channel_id=1, replica_groups=mesh['fsdp'=4,'expert'=32] {'expert'}, dimensions={0} | all-to-all | bytes 4194304 | tf_op jit(solution)/shard_map/all_to_all | solution.py:58
  272.2 0.3 reshape.149
  272.5 0.0 copy-start.1
  272.5 0.2 slice.162
  272.7 0.4 fusion.27
  273.1 0.9 fusion.3
  (18 shorter events, 0.3 us)
Async XLA Ops:
  0.0 3.5 %copy-start = (bf16[3,16,7168]{2,1,0:T(8,128)(2,1)S(1)}, bf16[3,16,7168]{2,1,0:T(8,128)(2,1)}, u32[]{:S(2)}) copy-start(bf16[3,16,7168]{2,1,0:T(8,128)(2,1)} %param.6) | copy-start | bytes 2064388
  4.3 0.7 copy-start.2
  147.7 5.0 %collective-permute-start = (f32[576,1024]{1,0:T(8,128)}, f32[576,1024]{1,0:T(8,128)}, u32[]{:S(2)}, u32[]{:S(2)}) collective-permute-start(f32[576,1024]{1,0:T(8,128)} %get-tuple-element.27), channel_id=1, source_target_pairs={{0,32},{32,0},{64,96},{96,64},{1,33},{33,1},{65,97},{97,65},{2,34}... | collective-permute-start | bytes 7077896 | tf_op jit(solution)/shard_map/ppermute | solution.py:202
  147.8 72.5 %all-to-all-start.1 = ((bf16[32,56,1024]{2,1,0:T(8,128)(2,1)}), bf16[32,56,1024]{2,1,0:T(8,128)(2,1)}, u32[]{:S(2)}, u32[]{:S(2)}) async-start(bf16[32,56,1024]{2,1,0:T(8,128)(2,1)} %get-tuple-element.28), calls=%async_computation.1 | async-start | bytes 7340032 | tf_op jit(solution)/shard_map/all_to_all | solution.py:58
  154.9 52.8 %collective-permute-start.1 = (bf16[576,512]{1,0:T(8,128)(2,1)S(1)}, bf16[576,512]{1,0:T(8,128)(2,1)S(1)}, u32[]{:S(2)}, u32[]{:S(2)}) collective-permute-start(bf16[576,512]{1,0:T(8,128)(2,1)S(1)} %pad_maximum_fusion), channel_id=1, source_target_pairs={{0,64},{64,0},{32,96},{96,32},{1,65},{65,1},{33,97},{97,33},{2,66}... | collective-permute-start | bytes 1769480 | tf_op jit(solution)/shard_map/ppermute | solution.py:207
  208.2 9.6 %collective-permute-start.2 = (bf16[576,256]{1,0:T(8,128)(2,1)S(1)}, bf16[576,256]{1,0:T(8,128)(2,1)S(1)}, u32[]{:S(2)}, u32[]{:S(2)}) collective-permute-start(bf16[576,256]{1,0:T(8,128)(2,1)S(1)} %fusion.10), channel_id=1, source_target_pairs={{0,64},{64,0},{32,96},{96,32},{1,65},{65,1},{33,97},{97,33},{2,66}... | collective-permute-start | bytes 884744 | tf_op jit(solution)/shard_map/ppermute | solution.py:209
  218.0 2.1 collective-permute-start.3
  272.5 1.5 copy-start.1

commit v2 on v1

v2 whole, which is shorter than its diff:
```python
import functools

import jax
import jax.numpy as jnp
from jax import lax
from jax.experimental import pallas as pl
from jax.experimental.pallas import tpu as pltpu
from jax.sharding import PartitionSpec as P


CORE_SWAP = ((0, 1), (1, 0), (2, 3), (3, 2))
CHIP_SWAP = ((0, 2), (2, 0), (1, 3), (3, 1))


def exchange(block):
    return lax.all_to_all(block, "expert", split_axis=0, concat_axis=0, tiled=True)


def swap_rows(block, pieces):
    size = block.shape[0] // pieces
    return jnp.concatenate(
        [lax.ppermute(block[i * size : (i + 1) * size], "fsdp", CHIP_SWAP) for i in range(pieces)]
    )


def pack_kernel(
    steps, rows, top, slot_count,
    at_ref, choices_ref, limit_ref, held_ref, tokens_ref, weights_ref,
    first_out, second_out, combine_ref, first_ref, second_ref, own, sems,
):
    experts, _, columns = weights_ref.shape
    wide = columns // 3 * 2
    share = own.shape[1]
    main = 16 * experts
    total = experts * steps * slot_count
    parts = 4
    some = [pl.ds(i * (experts // parts), experts // parts) for i in range(parts)]
    arriving, leaving = [], []
    for i in range(parts):
        inner = first_ref.at[some[i], :, pl.ds(0, wide)]
        arriving.append(
            pltpu.make_async_copy(weights_ref.at[some[i], :, pl.ds(0, wide)], inner, sems.at[0, i])
        )
        leaving.append(
            pltpu.make_async_copy(inner, first_out.at[some[i], :, pl.ds(0, wide)], sems.at[1, i])
        )
    for i in range(parts):
        arriving.append(
            pltpu.make_async_copy(
                weights_ref.at[some[i], :, pl.ds(wide, columns - wide)], second_ref.at[some[i]], sems.at[2, i]
            )
        )
        leaving.append(
            pltpu.make_async_copy(second_ref.at[some[i]], second_out.at[some[i]], sems.at[3, i])
        )
    start = pl.multiple_of(at_ref[0] * share, 128)
    fetch = pltpu.make_async_copy(tokens_ref.at[:, pl.ds(start, share)], own, sems.at[4, 0])
    fetch.start()
    for copy in arriving:
        copy.start()

    count = steps * rows * top
    ids = choices_ref[0:1, :].astype(jnp.int32)
    square = lax.broadcasted_iota(jnp.int32, (experts, experts), 1)
    diagonal = lax.broadcasted_iota(jnp.int32, (experts, experts), 0) == square
    held = jnp.sum(
        jnp.where(diagonal, held_ref[...].astype(jnp.float32), 0.0), axis=1, keepdims=True
    ).astype(jnp.int32)
    hot = held == ids
    hot32 = hot.astype(jnp.float32)
    before_of = lax.broadcasted_iota(jnp.int32, (count, count), 0)
    number = lax.broadcasted_iota(jnp.int32, (count, count), 1)
    per_step = rows * top
    earlier = (before_of < number) & (before_of >= number - (number & (per_step - 1)))
    before = jnp.dot(
        hot.astype(jnp.bfloat16), earlier.astype(jnp.bfloat16), preferred_element_type=jnp.float32
    )
    position = jnp.sum(before * hot32, axis=0, keepdims=True).astype(jnp.int32)
    named = held == square
    limit_of = jnp.sum(
        jnp.where(named, limit_ref[...].astype(jnp.float32), 0.0), axis=1, keepdims=True
    )
    limit = jnp.sum(hot32 * limit_of, axis=0, keepdims=True).astype(jnp.int32)
    holder = lax.broadcasted_iota(jnp.int32, (experts, count), 0).astype(jnp.float32)
    owner = jnp.sum(hot32 * holder, axis=0, keepdims=True).astype(jnp.int32)
    choice = lax.broadcasted_iota(jnp.int32, (1, count), 1)
    within = lax.shift_right_logical(choice, per_step.bit_length() - 1) * slot_count + position
    slot = jnp.where(within < 16, owner * 16 + within, main + owner * 2 + within - 16)
    slot = jnp.where(position < limit, slot, -1)

    row_of = lax.shift_right_logical(
        lax.broadcasted_iota(jnp.int32, (count, steps * rows), 0), top.bit_length() - 1
    )
    row_hot = (row_of == lax.broadcasted_iota(jnp.int32, (count, steps * rows), 1)).astype(jnp.bfloat16)

    def match(size, of):
        return (of(lax.broadcasted_iota(jnp.int32, (size, count), 0)) == slot).astype(jnp.bfloat16)

    top_match = match(main, lambda i: i)
    last_match = match(total - main, lambda i: i + main)
    tail_match = match(8 * experts, lambda i: main + lax.shift_right_logical(i, 2))
    choice_row = lax.shift_right_logical(
        lax.broadcasted_iota(jnp.int32, (steps * rows, count), 1), top.bit_length() - 1
    )
    here = choice_row == lax.broadcasted_iota(jnp.int32, (steps * rows, count), 0)
    weighted = jnp.where(here, choices_ref[1:2, :], 0.0).astype(jnp.bfloat16)
    contract = (((1,), (1,)), ((), ()))
    combine_ref[:, :main] = lax.dot_general(
        weighted, top_match, contract, preferred_element_type=jnp.float32
    ).astype(jnp.bfloat16)
    combine_ref[:, main:] = lax.dot_general(
        weighted, last_match, contract, preferred_element_type=jnp.float32
    ).astype(jnp.bfloat16)
    send_top = jnp.dot(top_match, row_hot, preferred_element_type=jnp.float32).astype(jnp.bfloat16)
    send_tail = jnp.dot(tail_match, row_hot, preferred_element_type=jnp.float32)
    piece_of = lax.broadcasted_iota(jnp.int32, (8 * experts, steps * rows), 0) & 3

    for here_now, onward in zip(arriving, leaving, strict=True):
        here_now.wait()
        onward.start()
    fetch.wait()
    for b in range(3):
        width = min(640, share - 640 * b)
        piece = jnp.dot(
            send_top, own[:, 640 * b : 640 * b + width], preferred_element_type=jnp.float32
        ).astype(jnp.bfloat16)
        first_ref[:, 16 * b : 16 * b + 16, wide : wide + width] = piece.reshape(experts, 16, width)
    zeros = jnp.zeros((experts, 24, 128), jnp.bfloat16)
    first_ref[:, 32:56, wide + 512 :] = zeros
    rest = jnp.zeros((8 * experts, 512), jnp.float32)
    for q in range(4):
        width = min(512, share - 512 * q)
        picked = jnp.where(piece_of == q, send_tail, 0.0).astype(jnp.bfloat16)
        piece = jnp.dot(picked, own[:, 512 * q : 512 * q + width], preferred_element_type=jnp.float32)
        if width < 512:
            piece = jnp.concatenate([piece, jnp.zeros((8 * experts, 512 - width), jnp.float32)], axis=1)
        rest = rest + piece
    first_ref[:, 48:56, wide : wide + 512] = rest.astype(jnp.bfloat16).reshape(experts, 8, 512)
    beside = pl.ds(wide, first_ref.shape[2] - wide)
    last = pltpu.make_async_copy(
        first_ref.at[:, :, beside], first_out.at[:, :, beside], sems.at[4, 1]
    )
    last.start()
    for copy in leaving:
        copy.wait()
    last.wait()


def pack(fsdp_at, tokens, route_ids, gate_values, cap_limit, update_ids, weights, slot_count, share):
    steps, rows, top = route_ids.shape
    experts, local, columns = weights.shape
    wide = columns // 3 * 2
    count = steps * rows * top
    vmem = pl.BlockSpec(memory_space=pltpu.VMEM)
    hbm = pl.BlockSpec(memory_space=pltpu.HBM)
    return pl.pallas_call(
        functools.partial(pack_kernel, steps, rows, top, slot_count),
        in_specs=[pl.BlockSpec(memory_space=pltpu.SMEM), vmem, vmem, vmem, hbm, hbm],
        out_specs=[hbm, hbm, vmem],
        out_shape=[
            jax.ShapeDtypeStruct((experts, local, wide + 640), weights.dtype),
            jax.ShapeDtypeStruct((experts, local, columns - wide), weights.dtype),
            jax.ShapeDtypeStruct((steps * rows, experts * steps * slot_count), jnp.bfloat16),
        ],
        scratch_shapes=[
            pltpu.VMEM((experts, local, wide + 640), weights.dtype),
            pltpu.VMEM((experts, local, columns - wide), weights.dtype),
            pltpu.VMEM((steps * rows, share), jnp.bfloat16),
            pltpu.SemaphoreType.DMA((5, 4)),
        ],
        compiler_params=pltpu.CompilerParams(vmem_limit_bytes=56 << 20),
        name="pack",
    )(
        fsdp_at.reshape(1),
        jnp.stack([route_ids.astype(jnp.float32), gate_values.astype(jnp.float32)]).reshape(2, count),
        cap_limit.reshape(1, experts),
        update_ids.reshape(1, experts),
        tokens.reshape(steps * rows, tokens.shape[2]),
        weights,
    )


def gate_up_kernel(core_ref, arrived_ref, passed_ref, kept_ref, weights, rows, tail, sems):
    experts, local, _ = arrived_ref.shape
    quarter = weights.shape[3]
    wide = 4 * quarter
    share = rows.shape[2]
    main = experts * 16
    core = core_ref[0]
    copies = [
        pltpu.make_async_copy(
            arrived_ref.at[:, pl.ds(16 * b, 16), pl.ds(wide, w)],
            rows.at[:, :, pl.ds(640 * b, w)],
            sems.at[b],
        )
        for b, w in enumerate((640, 640, share - 1280))
    ]
    copies.append(
        pltpu.make_async_copy(arrived_ref.at[:, pl.ds(48, 8), pl.ds(wide, 512)], tail, sems.at[3])
    )
    starts = [(1 - core) * quarter, (1 - core) * quarter + 2 * quarter]
    starts += [core * quarter, core * quarter + 2 * quarter]
    for i, start in enumerate(starts):
        copies.append(
            pltpu.make_async_copy(
                arrived_ref.at[:, :, pl.ds(pl.multiple_of(start, quarter), quarter)],
                weights.at[i],
                sems.at[4 + i],
            )
        )
    for copy in copies:
        copy.start()
    for copy in copies[:4]:
        copy.wait()
    top = rows[...].reshape(main, share)
    flat = tail[...].reshape(experts * 8, 512)
    at = lax.broadcasted_iota(jnp.int32, (2 * experts, 8 * experts), 0)
    of = lax.broadcasted_iota(jnp.int32, (2 * experts, 8 * experts), 1)
    pieces = []
    for q in range(4):
        pick = (of == at * 4 + q).astype(jnp.bfloat16)
        pieces.append(jnp.dot(pick, flat, preferred_element_type=jnp.float32).astype(jnp.bfloat16))
    last = jnp.concatenate(pieces, axis=1)[:, :share]
    for i in range(4):
        copies[4 + i].wait()
        block = weights[i].reshape(experts * local, quarter)
        out_ref = passed_ref if i < 2 else kept_ref
        columns = pl.ds((i % 2) * quarter, quarter)
        out_ref[:main, columns] = jnp.dot(top, block, preferred_element_type=jnp.float32)
        out_ref[main:, columns] = jnp.dot(last, block, preferred_element_type=jnp.float32)


def gate_up(core, arrived, hidden, share):
    experts, local, _ = arrived.shape
    slots = experts * 18
    quarter = hidden // 2
    out = jax.ShapeDtypeStruct((slots, hidden), jnp.float32)
    return pl.pallas_call(
        gate_up_kernel,
        in_specs=[
            pl.BlockSpec(memory_space=pltpu.SMEM),
            pl.BlockSpec(memory_space=pltpu.HBM),
        ],
        out_specs=[pl.BlockSpec(memory_space=pltpu.VMEM)] * 2,
        out_shape=[out, out],
        scratch_shapes=[
            pltpu.VMEM((4, experts, local, quarter), jnp.bfloat16),
            pltpu.VMEM((experts, 16, share), jnp.bfloat16),
            pltpu.VMEM((experts, 8, 512), jnp.bfloat16),
            pltpu.SemaphoreType.DMA((8,)),
        ],
        compiler_params=pltpu.CompilerParams(vmem_limit_bytes=54 << 20),
        cost_estimate=pl.CostEstimate(
            flops=2 * slots * share * 2 * hidden,
            bytes_accessed=2 * arrived.size + 8 * slots * hidden,
            transcendentals=0,
        ),
        name="gate_up",
    )(core, arrived)


def layer(tokens, route_ids, gate_values, cap_limit, update_ids, expert_weights):
    steps, rows, width = tokens.shape
    experts, _, _ = expert_weights.shape
    fsdp_count = lax.axis_size("fsdp")
    fsdp_at = lax.axis_index("fsdp").astype(jnp.int32)
    slot_count = 6
    hidden = expert_weights.shape[2] // 3
    half = hidden // 2
    quarter = half // 2
    share = width // fsdp_count
    main = experts * 16

    outgoing, down_raw, combine = pack(
        fsdp_at, tokens, route_ids, gate_values, cap_limit, update_ids, expert_weights, slot_count, share
    )
    core = (fsdp_at % 2).astype(jnp.int32)
    upper = fsdp_at // 2 == 1
    second = core == 1
    outgoing, down_raw, combine, core, upper, second = lax.optimization_barrier(
        (outgoing, down_raw, combine, core, upper, second)
    )
    arrived = exchange(outgoing)
    arrived, down_raw = lax.optimization_barrier((arrived, down_raw))
    down = exchange(down_raw).reshape(share, hidden)

    passed, kept = gate_up(core.reshape(1), arrived, hidden, share)
    kept = kept + lax.ppermute(passed, "fsdp", CORE_SWAP)
    g0, g1, u0, u1 = (kept[:, i * quarter : (i + 1) * quarter] for i in range(4))
    send = jnp.concatenate([jnp.where(upper, g0, g1), jnp.where(upper, u0, u1)], axis=1)
    gate = jnp.where(upper, g1, g0)
    up = jnp.where(upper, u1, u0)
    across = swap_rows(send.astype(jnp.bfloat16), 6).astype(jnp.float32)
    act = (jax.nn.silu(gate + across[:, :quarter]) * (up + across[:, quarter:])).astype(jnp.bfloat16)
    other = swap_rows(act, 3)
    act = jnp.concatenate([jnp.where(upper, other, act), jnp.where(upper, act, other)], axis=1)
    other = lax.ppermute(act, "fsdp", CORE_SWAP)
    act = jnp.concatenate([jnp.where(second, other, act), jnp.where(second, act, other)], axis=1)
    out = lax.dot_general(
        act, down, (((1,), (1,)), ((), ())), preferred_element_type=jnp.float32
    ).astype(jnp.bfloat16)
    rest = out[main:].reshape(experts, 14, 256)
    rest = jnp.pad(rest, ((0, 0), (0, 2), (0, 0)))
    going = jnp.concatenate([out[:main].reshape(experts, 16, share), rest], axis=2)
    returned = exchange(going)
    mixed = jnp.dot(
        combine[:, :main],
        returned[:, :, :share].reshape(main, share),
        preferred_element_type=jnp.float32,
    ) + jnp.dot(
        combine[:, main:],
        returned[:, :14, share:].reshape(experts * 2, share),
        preferred_element_type=jnp.float32,
    )
    return mixed.astype(jnp.bfloat16).reshape(steps, rows, share)


def solution(mesh):
    return jax.shard_map(
        layer,
        mesh=mesh,
        in_specs=(
            P(None, "expert", None),
            P(None, "expert", None),
            P(None, "expert", None),
            P(),
            P(),
            P(None, ("fsdp", "expert"), None),
        ),
        out_specs=P(None, "expert", "fsdp"),
        check_vma=False,
    )
```

time: 275 us -> 272 us (0.989)
  waiting for transfers between devices: 61.1 us -> 51.3 us
  starting transfers between devices: 8.34 us -> 17.1 us
    ppermute x2 -> x9, waiting for transfers between devices: 59.1 us -> 49.3 us  [swap_rows(): lax.ppermute(block[i * size:(i + 1) * size], 'fsdp', CHIP_SWAP)]
    ppermute x2 -> x9, starting transfers between devices: 3.33 us -> 11.8 us  [swap_rows(): lax.ppermute(block[i * size:(i + 1) * size], 'fsdp', CHIP_SWAP)]
  transfers between devices with their start and end apart: 5 -> 12, of which waited for: 3 -> 8; matrix products, arithmetic and copies ran while one was open for 1% -> 1% of each run, Pallas kernels for 0% -> 0%
where the time goes in v2:
time: 272 us; the launch traced here: 271 us
  blocking collectives  169 us (62%)
  waiting for transfers between devices  51.3 us (19%)
  Pallas kernels  20.6 us (8%)
  starting transfers between devices  17.1 us (6%)
  matrix products  5.65 us (2%)
  other arithmetic  4.69 us (2%)
    all_to_all x2, blocking collectives, exchange(): lax.all_to_all(block, 'expert', split_axis=0, concat_axis=0, tiled=True)  169 us
    ppermute x9, waiting for transfers between devices, swap_rows(): lax.ppermute(block[i * size:(i + 1) * size], 'fsdp', CHIP_SWAP)  49.3 us
    ppermute x9, starting transfers between devices, swap_rows(): lax.ppermute(block[i * size:(i + 1) * size], 'fsdp', CHIP_SWAP)  11.8 us
    pallas_call x1, Pallas kernels, pack(): pl.pallas_call(functools.partial(pack_kernel, steps, rows, top, slot_coun...  11.4 us
    pallas_call x1, Pallas kernels, gate_up(): pl.pallas_call(gate_up_kernel, in_specs=[pl.BlockSpec(memory_space=pltpu....  9.29 us
  transfers between devices with their start and end apart: 12, of which 8 were waited for; matrix products, arithmetic and copies ran while one was open for 1% of the time, Pallas kernels for 0%

profile of v2, /device:TPU:0, one launch (start us, length us, event | category | flops | bytes accessed | tf_op | source)
XLA Modules:
  0.0 271.1 jit_solution(7473931754334956378)
XLA Ops:
  0.0 0.7 convert_element_type.19
  0.7 0.1 copy.9
  0.8 0.1 stack.11
  0.9 0.8 copy.10
  1.6 0.1 reshape.50
  1.7 0.6 pad_maximum_fusion.2.choices_ref
  2.3 11.4 %pack.1 = (bf16[32,56,2688]{2,1,0:T(8,128)(2,1)}, bf16[32,56,1024]{2,1,0:T(8,128)(2,1)}, bf16[48,576]{1,0:T(8,128)(2,1)}) custom-call(s32[1]{0:T(128)} %bitcast.at_ref, f32[2,384]{1,0:T(2,128)} %pad_maximum_fusion.2.choices_ref, s32[1,32]{1,0:T(1,128)} %bitcast.15, s32[1,32]{1,0:T(1,128)} %bitcast.16, bf16[48,7168]{1,0:T(8,128)(2,1)} %bitcast.14, ...), custom_call_target="tpu_custom_call" | custom-call | tf_op jit(solution)/shard_map/pack/pallas_call | solution.py:156
  13.7 122.3 %all_to_all.15.arrived_ref = bf16[32,56,2688]{2,1,0:T(8,128)(2,1)} all-to-all(bf16[32,56,2688]{2,1,0:T(8,128)(2,1)} %get-tuple-element.25), channel_id=1, replica_groups=mesh['fsdp'=4,'expert'=32] {'expert'}, dimensions={0} | all-to-all | bytes 19267584 | tf_op jit(solution)/shard_map/all_to_all | solution.py:16
  136.0 9.3 %gate_up.1 = (f32[576,1024]{1,0:T(8,128)}, f32[576,1024]{1,0:T(8,128)}) custom-call(s32[1]{0:T(128)} %bitcast.4.core_ref, bf16[32,56,2688]{2,1,0:T(8,128)(2,1)} %all_to_all.15.arrived_ref), custom_call_target="tpu_custom_call" | custom-call | flops 4227858432 | bytes 14352384 | tf_op jit(solution)/shard_map/gate_up/pallas_call | solution.py:238
  145.3 0.1 collective-permute-start
  145.4 5.0 %all-to-all-start.1 = ((bf16[32,56,1024]{2,1,0:T(8,128)(2,1)}), bf16[32,56,1024]{2,1,0:T(8,128)(2,1)}, u32[]{:S(2)}, u32[]{:S(2)}) async-start(bf16[32,56,1024]{2,1,0:T(8,128)(2,1)} %get-tuple-element.30), calls=%async_computation.1 | async-start | bytes 7340032 | tf_op jit(solution)/shard_map/all_to_all | solution.py:16
  150.4 0.0 collective-permute-done
  150.4 2.1 add.24
  152.5 0.1 select_convert_fusion
  152.7 1.0 collective-permute-start.1
  153.7 1.1 collective-permute-start.6
  154.8 0.9 collective-permute-start.2
  155.7 1.1 collective-permute-start.3
  156.8 0.9 collective-permute-start.4
  157.7 31.6 %collective-permute-done.1 = bf16[96,512]{1,0:T(8,128)(2,1)S(1)} collective-permute-done((bf16[96,512]{1,0:T(8,128)(2,1)S(1)}, bf16[96,512]{1,0:T(8,128)(2,1)S(1)}, u32[]{:S(2)}, u32[]{:S(2)}) %collective-permute-start.1) | collective-permute-done | bytes 98336 | tf_op jit(solution)/shard_map/ppermute | solution.py:22
  189.3 2.2 collective-permute-start.5
  191.5 7.0 %collective-permute-done.2 = bf16[96,512]{1,0:T(8,128)(2,1)S(1)} collective-permute-done((bf16[96,512]{1,0:T(8,128)(2,1)S(1)}, bf16[96,512]{1,0:T(8,128)(2,1)S(1)}, u32[]{:S(2)}, u32[]{:S(2)}) %collective-permute-start.2) | collective-permute-done | bytes 98336 | tf_op jit(solution)/shard_map/ppermute | solution.py:22
  198.5 2.1 collective-permute-done.3
  200.6 2.1 collective-permute-done.4
  202.7 1.7 collective-permute-done.5
  204.4 0.0 collective-permute-done.6
  204.4 0.1 convert_element_type.20
  204.6 0.4 fusion.7
  205.0 2.6 collective-permute-start.7
  207.5 0.1 collective-permute-start.9
  207.6 1.9 collective-permute-start.8
  209.5 1.4 collective-permute-done.7
  210.9 3.6 %collective-permute-done.8 = bf16[192,256]{1,0:T(8,128)(2,1)S(1)} collective-permute-done((bf16[192,256]{1,0:T(8,128)(2,1)S(1)}, bf16[192,256]{1,0:T(8,128)(2,1)S(1)}, u32[]{:S(2)}, u32[]{:S(2)}) %collective-permute-start.8) | collective-permute-done | bytes 98336 | tf_op jit(solution)/shard_map/ppermute | solution.py:22
  214.5 0.0 collective-permute-done.9
  214.6 0.3 collective-permute-start.10
  214.9 2.0 collective-permute-done.10
  216.9 0.2 broadcast_select_fusion.1
  217.1 4.4 %convolution_convert_fusion = bf16[576,1792]{1,0:T(8,128)(2,1)S(1)} fusion(bf16[1792,1024]{1,0:T(8,128)(2,1)} %bitcast.5, bf16[576,512]{1,0:T(8,128)(2,1)S(1)} %get-tuple-element.34, bf16[576,512]{1,0:T(8,128)(2,1)S(1)} %get-tuple-element.33), kind=kOutput, calls=%fused_computation.2 | convolution fusion | flops 2117320704 | bytes 6914048 | tf_op jit(solution)/shard_map/dot_general | solution.py:299
  221.5 0.1 slice.103
  221.7 0.3 reshape.46
  221.9 0.3 fusion.2
  222.2 46.8 %all_to_all.16 = bf16[32,16,2048]{2,1,0:T(8,128)(2,1)S(1)} all-to-all(bf16[32,16,2048]{2,1,0:T(8,128)(2,1)S(1)} %fusion.2), channel_id=1, replica_groups=mesh['fsdp'=4,'expert'=32] {'expert'}, dimensions={0} | all-to-all | bytes 4194304 | tf_op jit(solution)/shard_map/all_to_all | solution.py:16
  269.0 0.0 copy-start.1
  269.0 0.3 reshape.48
  269.3 0.2 slice.105
  269.4 0.4 copy-done.1
  269.8 0.4 fusion.13
  270.3 0.9 fusion.1
  (18 shorter events, 0.3 us)
Async XLA Ops:
  145.3 5.1 %copy-start = (f32[576,1024]{1,0:T(8,128)S(1)}, f32[576,1024]{1,0:T(8,128)}, u32[]{:S(2)}) copy-start(f32[576,1024]{1,0:T(8,128)} %get-tuple-element.28) | copy-start | bytes 7077892
  145.3 5.1 %collective-permute-start = (f32[576,1024]{1,0:T(8,128)}, f32[576,1024]{1,0:T(8,128)}, u32[]{:S(2)}, u32[]{:S(2)}) collective-permute-start(f32[576,1024]{1,0:T(8,128)} %get-tuple-element.29), channel_id=1, source_target_pairs={{0,32},{32,0},{64,96},{96,64},{1,33},{33,1},{65,97},{97,65},{2,34}... | collective-permute-start | bytes 7077896 | tf_op jit(solution)/shard_map/ppermute | solution.py:288
  145.4 71.7 %all-to-all-start.1 = ((bf16[32,56,1024]{2,1,0:T(8,128)(2,1)}), bf16[32,56,1024]{2,1,0:T(8,128)(2,1)}, u32[]{:S(2)}, u32[]{:S(2)}) async-start(bf16[32,56,1024]{2,1,0:T(8,128)(2,1)} %get-tuple-element.30), calls=%async_computation.1 | async-start | bytes 7340032 | tf_op jit(solution)/shard_map/all_to_all | solution.py:16
  152.7 36.6 %collective-permute-start.1 = (bf16[96,512]{1,0:T(8,128)(2,1)S(1)}, bf16[96,512]{1,0:T(8,128)(2,1)S(1)}, u32[]{:S(2)}, u32[]{:S(2)}) collective-permute-start(bf16[96,512]{1,0:T(8,128)(2,1)S(1)} %get-tuple-element.38), channel_id=1, source_target_pairs={{0,64},{64,0},{32,96},{96,32},{1,65},{65,1},{33,97},{97,33},{2,66}... | collective-permute-start | bytes 294920 | tf_op jit(solution)/shard_map/ppermute | solution.py:22
  153.7 50.7 %collective-permute-start.6 = (bf16[96,512]{1,0:T(8,128)(2,1)S(1)}, bf16[96,512]{1,0:T(8,128)(2,1)S(1)}, u32[]{:S(2)}, u32[]{:S(2)}) collective-permute-start(bf16[96,512]{1,0:T(8,128)(2,1)S(1)} %get-tuple-element.37), channel_id=1, source_target_pairs={{0,64},{64,0},{32,96},{96,32},{1,65},{65,1},{33,97},{97,33},{2,66}... | collective-permute-start | bytes 294920 | tf_op jit(solution)/shard_map/ppermute | solution.py:22
  154.8 43.6 %collective-permute-start.2 = (bf16[96,512]{1,0:T(8,128)(2,1)S(1)}, bf16[96,512]{1,0:T(8,128)(2,1)S(1)}, u32[]{:S(2)}, u32[]{:S(2)}) collective-permute-start(bf16[96,512]{1,0:T(8,128)(2,1)S(1)} %get-tuple-element.39), channel_id=1, source_target_pairs={{0,64},{64,0},{32,96},{96,32},{1,65},{65,1},{33,97},{97,33},{2,66}... | collective-permute-start | bytes 294920 | tf_op jit(solution)/shard_map/ppermute | solution.py:22
  155.7 44.8 %collective-permute-start.3 = (bf16[96,512]{1,0:T(8,128)(2,1)S(1)}, bf16[96,512]{1,0:T(8,128)(2,1)S(1)}, u32[]{:S(2)}, u32[]{:S(2)}) collective-permute-start(bf16[96,512]{1,0:T(8,128)(2,1)S(1)} %get-tuple-element.40), channel_id=1, source_target_pairs={{0,64},{64,0},{32,96},{96,32},{1,65},{65,1},{33,97},{97,33},{2,66}... | collective-permute-start | bytes 294920 | tf_op jit(solution)/shard_map/ppermute | solution.py:22
  156.8 45.8 %collective-permute-start.4 = (bf16[96,512]{1,0:T(8,128)(2,1)S(1)}, bf16[96,512]{1,0:T(8,128)(2,1)S(1)}, u32[]{:S(2)}, u32[]{:S(2)}) collective-permute-start(bf16[96,512]{1,0:T(8,128)(2,1)S(1)} %get-tuple-element.41), channel_id=1, source_target_pairs={{0,64},{64,0},{32,96},{96,32},{1,65},{65,1},{33,97},{97,33},{2,66}... | collective-permute-start | bytes 294920 | tf_op jit(solution)/shard_map/ppermute | solution.py:22
  189.3 15.1 %collective-permute-start.5 = (bf16[96,512]{1,0:T(8,128)(2,1)S(1)}, bf16[96,512]{1,0:T(8,128)(2,1)S(1)}, u32[]{:S(2)}, u32[]{:S(2)}) collective-permute-start(bf16[96,512]{1,0:T(8,128)(2,1)S(1)} %get-tuple-element.42), channel_id=1, source_target_pairs={{0,64},{64,0},{32,96},{96,32},{1,65},{65,1},{33,97},{97,33},{2,66}... | collective-permute-start | bytes 294920 | tf_op jit(solution)/shard_map/ppermute | solution.py:22
  205.0 5.9 %collective-permute-start.7 = (bf16[192,256]{1,0:T(8,128)(2,1)S(1)}, bf16[192,256]{1,0:T(8,128)(2,1)S(1)}, u32[]{:S(2)}, u32[]{:S(2)}) collective-permute-start(bf16[192,256]{1,0:T(8,128)(2,1)S(1)} %get-tuple-element.45), channel_id=1, source_target_pairs={{0,64},{64,0},{32,96},{96,32},{1,65},{65,1},{33,97},{97,33},{2,66}... | collective-permute-start | bytes 294920 | tf_op jit(solution)/shard_map/ppermute | solution.py:22
  207.5 7.0 %collective-permute-start.9 = (bf16[192,256]{1,0:T(8,128)(2,1)S(1)}, bf16[192,256]{1,0:T(8,128)(2,1)S(1)}, u32[]{:S(2)}, u32[]{:S(2)}) collective-permute-start(bf16[192,256]{1,0:T(8,128)(2,1)S(1)} %get-tuple-element.43), channel_id=1, source_target_pairs={{0,64},{64,0},{32,96},{96,32},{1,65},{65,1},{33,97},{97,33},{2,66}... | collective-permute-start | bytes 294920 | tf_op jit(solution)/shard_map/ppermute | solution.py:22
  207.6 6.9 %collective-permute-start.8 = (bf16[192,256]{1,0:T(8,128)(2,1)S(1)}, bf16[192,256]{1,0:T(8,128)(2,1)S(1)}, u32[]{:S(2)}, u32[]{:S(2)}) collective-permute-start(bf16[192,256]{1,0:T(8,128)(2,1)S(1)} %get-tuple-element.44), channel_id=1, source_target_pairs={{0,64},{64,0},{32,96},{96,32},{1,65},{65,1},{33,97},{97,33},{2,66}... | collective-permute-start | bytes 294920 | tf_op jit(solution)/shard_map/ppermute | solution.py:22
  214.6 2.3 collective-permute-start.10
  269.0 0.8 copy-start.1

commit v3 on v2

--- a/solution.py
+++ b/solution.py
@@ -25,7 +25,7 @@
 
 def pack_kernel(
     steps, rows, top, slot_count,
-    at_ref, choices_ref, limit_ref, held_ref, tokens_ref, weights_ref,
+    at_ref, ids_ref, gates_ref, limit_ref, held_ref, tokens_ref, weights_ref,
     first_out, second_out, combine_ref, first_ref, second_ref, own, sems,
 ):
     experts, _, columns = weights_ref.shape
@@ -60,7 +60,29 @@
         copy.start()
 
     count = steps * rows * top
-    ids = choices_ref[0:1, :].astype(jnp.int32)
+    per_step = rows * top
+    top_bits = top.bit_length() - 1
+    step_bits = per_step.bit_length() - 1
+
+    def in_order(values):
+        named_row = lax.broadcasted_iota(jnp.int32, (rows, count), 0)
+        spread_at = lax.broadcasted_iota(jnp.int32, (rows, count), 1)
+        spread = (lax.shift_right_logical(spread_at, top_bits) & (rows - 1)) == named_row
+        wide_values = jnp.dot(
+            values.astype(jnp.bfloat16), spread.astype(jnp.bfloat16), preferred_element_type=jnp.float32
+        )
+        line = lax.broadcasted_iota(jnp.int32, (steps * top, count), 0)
+        column = lax.broadcasted_iota(jnp.int32, (steps * top, count), 1)
+        own_line = lax.shift_right_logical(column, step_bits) * top + (column & (top - 1))
+        return jnp.sum(jnp.where(line == own_line, wide_values, 0.0), axis=0, keepdims=True)
+
+    def forward(lines):
+        for i in lines:
+            arriving[i].wait()
+            leaving[i].start()
+
+    ids = in_order(ids_ref[...].astype(jnp.float32)).astype(jnp.int32)
+    gates = in_order(gates_ref[...])
     square = lax.broadcasted_iota(jnp.int32, (experts, experts), 1)
     diagonal = lax.broadcasted_iota(jnp.int32, (experts, experts), 0) == square
     held = jnp.sum(
@@ -70,12 +92,12 @@
     hot32 = hot.astype(jnp.float32)
     before_of = lax.broadcasted_iota(jnp.int32, (count, count), 0)
     number = lax.broadcasted_iota(jnp.int32, (count, count), 1)
-    per_step = rows * top
     earlier = (before_of < number) & (before_of >= number - (number & (per_step - 1)))
     before = jnp.dot(
         hot.astype(jnp.bfloat16), earlier.astype(jnp.bfloat16), preferred_element_type=jnp.float32
     )
     position = jnp.sum(before * hot32, axis=0, keepdims=True).astype(jnp.int32)
+    forward(range(0, 3))
     named = held == square
     limit_of = jnp.sum(
         jnp.where(named, limit_ref[...].astype(jnp.float32), 0.0), axis=1, keepdims=True
@@ -84,10 +106,11 @@
     holder = lax.broadcasted_iota(jnp.int32, (experts, count), 0).astype(jnp.float32)
     owner = jnp.sum(hot32 * holder, axis=0, keepdims=True).astype(jnp.int32)
     choice = lax.broadcasted_iota(jnp.int32, (1, count), 1)
-    within = lax.shift_right_logical(choice, per_step.bit_length() - 1) * slot_count + position
+    within = lax.shift_right_logical(choice, step_bits) * slot_count + position
     slot = jnp.where(within < 16, owner * 16 + within, main + owner * 2 + within - 16)
     slot = jnp.where(position < limit, slot, -1)
 
+    forward(range(3, 5))
     row_of = lax.shift_right_logical(
         lax.broadcasted_iota(jnp.int32, (count, steps * rows), 0), top.bit_length() - 1
     )
@@ -103,7 +126,7 @@
         lax.broadcasted_iota(jnp.int32, (steps * rows, count), 1), top.bit_length() - 1
     )
     here = choice_row == lax.broadcasted_iota(jnp.int32, (steps * rows, count), 0)
-    weighted = jnp.where(here, choices_ref[1:2, :], 0.0).astype(jnp.bfloat16)
+    weighted = jnp.where(here, gates, 0.0).astype(jnp.bfloat16)
     contract = (((1,), (1,)), ((), ()))
     combine_ref[:, :main] = lax.dot_general(
         weighted, top_match, contract, preferred_element_type=jnp.float32
@@ -111,13 +134,11 @@
     combine_ref[:, main:] = lax.dot_general(
         weighted, last_match, contract, preferred_element_type=jnp.float32
     ).astype(jnp.bfloat16)
+    forward(range(5, 2 * parts))
     send_top = jnp.dot(top_match, row_hot, preferred_element_type=jnp.float32).astype(jnp.bfloat16)
     send_tail = jnp.dot(tail_match, row_hot, preferred_element_type=jnp.float32)
     piece_of = lax.broadcasted_iota(jnp.int32, (8 * experts, steps * rows), 0) & 3
 
-    for here_now, onward in zip(arriving, leaving, strict=True):
-        here_now.wait()
-        onward.start()
     fetch.wait()
     for b in range(3):
         width = min(640, share - 640 * b)
@@ -150,12 +171,11 @@
     steps, rows, top = route_ids.shape
     experts, local, columns = weights.shape
     wide = columns // 3 * 2
-    count = steps * rows * top
     vmem = pl.BlockSpec(memory_space=pltpu.VMEM)
     hbm = pl.BlockSpec(memory_space=pltpu.HBM)
     return pl.pallas_call(
         functools.partial(pack_kernel, steps, rows, top, slot_count),
-        in_specs=[pl.BlockSpec(memory_space=pltpu.SMEM), vmem, vmem, vmem, hbm, hbm],
+        in_specs=[pl.BlockSpec(memory_space=pltpu.SMEM), vmem, vmem, vmem, vmem, hbm, hbm],
         out_specs=[hbm, hbm, vmem],
         out_shape=[
             jax.ShapeDtypeStruct((experts, local, wide + 640), weights.dtype),
@@ -172,7 +192,8 @@
         name="pack",
     )(
         fsdp_at.reshape(1),
-        jnp.stack([route_ids.astype(jnp.float32), gate_values.astype(jnp.float32)]).reshape(2, count),
+        route_ids.transpose(0, 2, 1).reshape(steps * top, rows),
+        gate_values.transpose(0, 2, 1).reshape(steps * top, rows),
         cap_limit.reshape(1, experts),
         update_ids.reshape(1, experts),
         tokens.reshape(steps * rows, tokens.shape[2]),

time: 272 us -> 268 us (0.985)
  no operation moved by 1% of the time
where the time goes in v3:
time: 268 us
  blocking collectives  168 us (63%)
  waiting for transfers between devices  49.5 us (18%)
  Pallas kernels  20.9 us (8%)
  starting transfers between devices  18.9 us (7%)
  matrix products  5.64 us (2%)
  other arithmetic  3.38 us (1%)
    all_to_all x2, blocking collectives, exchange(): lax.all_to_all(block, 'expert', split_axis=0, concat_axis=0, tiled=True)  168 us
    ppermute x9, waiting for transfers between devices, swap_rows(): lax.ppermute(block[i * size:(i + 1) * size], 'fsdp', CHIP_SWAP)  47.5 us
    ppermute x9, starting transfers between devices, swap_rows(): lax.ppermute(block[i * size:(i + 1) * size], 'fsdp', CHIP_SWAP)  13.6 us
    pallas_call x1, Pallas kernels, pack(): pl.pallas_call(functools.partial(pack_kernel, steps, rows, top, slot_coun...  11.6 us
    pallas_call x1, Pallas kernels, gate_up(): pl.pallas_call(gate_up_kernel, in_specs=[pl.BlockSpec(memory_space=pltpu....  9.28 us
  transfers between devices with their start and end apart: 12, of which 8 were waited for; matrix products, arithmetic and copies ran while one was open for 1% of the time, Pallas kernels for 0%

profile of v3, /device:TPU:0, one launch (start us, length us, event | category | flops | bytes accessed | tf_op | source)
XLA Modules:
  0.0 267.6 jit_solution(5393222448192736582)
XLA Ops:
  0.0 11.6 %pack.1 = (bf16[32,56,2688]{2,1,0:T(8,128)(2,1)}, bf16[32,56,1024]{2,1,0:T(8,128)(2,1)}, bf16[48,576]{1,0:T(8,128)(2,1)}) custom-call(s32[1]{0:T(128)} %bitcast.at_ref, s32[24,16]{1,0:T(8,128)} %bitcast.21, bf16[24,16]{1,0:T(8,128)(2,1)} %bitcast.22, s32[1,32]{1,0:T(1,128)} %bitcast.23, s32[1,32]{1,0:T(1,128)} %bitcast.24, bf16[48,7168]{1,0:T(8,128)(2,1)} %bitcast.20, ...), custom_call_target="tpu_custom_call" | custom-call | tf_op jit(solution)/shard_map/pack/pallas_call | solution.py:176
  11.6 122.3 %all_to_all.15.arrived_ref = bf16[32,56,2688]{2,1,0:T(8,128)(2,1)} all-to-all(bf16[32,56,2688]{2,1,0:T(8,128)(2,1)} %get-tuple-element.25), channel_id=1, replica_groups=mesh['fsdp'=4,'expert'=32] {'expert'}, dimensions={0} | all-to-all | bytes 19267584 | tf_op jit(solution)/shard_map/all_to_all | solution.py:16
  133.9 9.3 %gate_up.1 = (f32[576,1024]{1,0:T(8,128)}, f32[576,1024]{1,0:T(8,128)}) custom-call(s32[1]{0:T(128)} %bitcast.8.core_ref, bf16[32,56,2688]{2,1,0:T(8,128)(2,1)} %all_to_all.15.arrived_ref), custom_call_target="tpu_custom_call" | custom-call | flops 4227858432 | bytes 14352384 | tf_op jit(solution)/shard_map/gate_up/pallas_call | solution.py:259
  143.2 0.0 copy-start
  143.2 0.1 collective-permute-start
  143.3 5.0 %all-to-all-start.1 = ((bf16[32,56,1024]{2,1,0:T(8,128)(2,1)}), bf16[32,56,1024]{2,1,0:T(8,128)(2,1)}, u32[]{:S(2)}, u32[]{:S(2)}) async-start(bf16[32,56,1024]{2,1,0:T(8,128)(2,1)} %get-tuple-element.30), calls=%async_computation.1 | async-start | bytes 7340032 | tf_op jit(solution)/shard_map/all_to_all | solution.py:16
  148.3 0.0 collective-permute-done
  148.3 0.0 copy-done
  148.3 2.1 add.24
  150.4 0.1 select_convert_fusion
  150.6 0.8 collective-permute-start.1
  151.4 1.3 collective-permute-start.6
  152.7 0.7 collective-permute-start.2
  153.4 1.3 collective-permute-start.3
  154.7 0.7 collective-permute-start.4
  155.4 29.8 %collective-permute-done.1 = bf16[96,512]{1,0:T(8,128)(2,1)S(1)} collective-permute-done((bf16[96,512]{1,0:T(8,128)(2,1)S(1)}, bf16[96,512]{1,0:T(8,128)(2,1)S(1)}, u32[]{:S(2)}, u32[]{:S(2)}) %collective-permute-start.1) | collective-permute-done | bytes 98336 | tf_op jit(solution)/shard_map/ppermute | solution.py:22
  185.2 4.2 %collective-permute-start.5 = (bf16[96,512]{1,0:T(8,128)(2,1)S(1)}, bf16[96,512]{1,0:T(8,128)(2,1)S(1)}, u32[]{:S(2)}, u32[]{:S(2)}) collective-permute-start(bf16[96,512]{1,0:T(8,128)(2,1)S(1)} %get-tuple-element.42), channel_id=1, source_target_pairs={{0,64},{64,0},{32,96},{96,32},{1,65},{65,1},{33,97},{97,33},{2,66}... | collective-permute-start | bytes 294920 | tf_op jit(solution)/shard_map/ppermute | solution.py:22
  189.4 6.9 %collective-permute-done.2 = bf16[96,512]{1,0:T(8,128)(2,1)S(1)} collective-permute-done((bf16[96,512]{1,0:T(8,128)(2,1)S(1)}, bf16[96,512]{1,0:T(8,128)(2,1)S(1)}, u32[]{:S(2)}, u32[]{:S(2)}) %collective-permute-start.2) | collective-permute-done | bytes 98336 | tf_op jit(solution)/shard_map/ppermute | solution.py:22
  196.3 2.1 collective-permute-done.3
  198.4 2.1 collective-permute-done.4
  200.5 1.8 collective-permute-done.5
  202.3 0.0 collective-permute-done.6
  202.3 0.1 convert_element_type.15
  202.5 0.4 fusion.7
  202.9 2.6 collective-permute-start.7
  205.4 0.1 collective-permute-start.9
  205.5 1.9 collective-permute-start.8
  207.5 1.4 collective-permute-done.7
  208.8 3.6 %collective-permute-done.8 = bf16[192,256]{1,0:T(8,128)(2,1)S(1)} collective-permute-done((bf16[192,256]{1,0:T(8,128)(2,1)S(1)}, bf16[192,256]{1,0:T(8,128)(2,1)S(1)}, u32[]{:S(2)}, u32[]{:S(2)}) %collective-permute-start.8) | collective-permute-done | bytes 98336 | tf_op jit(solution)/shard_map/ppermute | solution.py:22
  212.4 0.0 collective-permute-done.9
  212.5 0.3 collective-permute-start.10
  212.8 2.0 collective-permute-done.10
  214.8 0.2 broadcast_select_fusion.1
  215.0 0.0 all-to-all-done.1
  215.0 4.4 %convolution_convert_fusion = bf16[576,1792]{1,0:T(8,128)(2,1)S(1)} fusion(bf16[1792,1024]{1,0:T(8,128)(2,1)} %bitcast.9, bf16[576,512]{1,0:T(8,128)(2,1)S(1)} %get-tuple-element.34, bf16[576,512]{1,0:T(8,128)(2,1)S(1)} %get-tuple-element.33), kind=kOutput, calls=%fused_computation.2 | convolution fusion | flops 2117320704 | bytes 6914048 | tf_op jit(solution)/shard_map/dot_general | solution.py:320
  219.4 0.1 slice.103
  219.6 0.3 reshape.48
  219.8 0.3 fusion.2
  220.1 45.4 %all_to_all.16 = bf16[32,16,2048]{2,1,0:T(8,128)(2,1)S(1)} all-to-all(bf16[32,16,2048]{2,1,0:T(8,128)(2,1)S(1)} %fusion.2), channel_id=1, replica_groups=mesh['fsdp'=4,'expert'=32] {'expert'}, dimensions={0} | all-to-all | bytes 4194304 | tf_op jit(solution)/shard_map/all_to_all | solution.py:16
  265.5 0.0 copy-start.1
  265.5 0.3 reshape.50
  265.8 0.2 slice.105
  265.9 0.4 copy-done.1
  266.3 0.4 fusion.13
  266.8 0.9 fusion.1
  (15 shorter events, 0.3 us)
Async XLA Ops:
  143.2 5.1 %copy-start = (f32[576,1024]{1,0:T(8,128)S(1)}, f32[576,1024]{1,0:T(8,128)}, u32[]{:S(2)}) copy-start(f32[576,1024]{1,0:T(8,128)} %get-tuple-element.28) | copy-start | bytes 7077892
  143.2 5.1 %collective-permute-start = (f32[576,1024]{1,0:T(8,128)}, f32[576,1024]{1,0:T(8,128)}, u32[]{:S(2)}, u32[]{:S(2)}) collective-permute-start(f32[576,1024]{1,0:T(8,128)} %get-tuple-element.29), channel_id=1, source_target_pairs={{0,32},{32,0},{64,96},{96,64},{1,33},{33,1},{65,97},{97,65},{2,34}... | collective-permute-start | bytes 7077896 | tf_op jit(solution)/shard_map/ppermute | solution.py:309
  143.3 71.7 %all-to-all-start.1 = ((bf16[32,56,1024]{2,1,0:T(8,128)(2,1)}), bf16[32,56,1024]{2,1,0:T(8,128)(2,1)}, u32[]{:S(2)}, u32[]{:S(2)}) async-start(bf16[32,56,1024]{2,1,0:T(8,128)(2,1)} %get-tuple-element.30), calls=%async_computation.1 | async-start | bytes 7340032 | tf_op jit(solution)/shard_map/all_to_all | solution.py:16
  150.6 34.6 %collective-permute-start.1 = (bf16[96,512]{1,0:T(8,128)(2,1)S(1)}, bf16[96,512]{1,0:T(8,128)(2,1)S(1)}, u32[]{:S(2)}, u32[]{:S(2)}) collective-permute-start(bf16[96,512]{1,0:T(8,128)(2,1)S(1)} %get-tuple-element.38), channel_id=1, source_target_pairs={{0,64},{64,0},{32,96},{96,32},{1,65},{65,1},{33,97},{97,33},{2,66}... | collective-permute-start | bytes 294920 | tf_op jit(solution)/shard_map/ppermute | solution.py:22
  151.4 50.9 %collective-permute-start.6 = (bf16[96,512]{1,0:T(8,128)(2,1)S(1)}, bf16[96,512]{1,0:T(8,128)(2,1)S(1)}, u32[]{:S(2)}, u32[]{:S(2)}) collective-permute-start(bf16[96,512]{1,0:T(8,128)(2,1)S(1)} %get-tuple-element.37), channel_id=1, source_target_pairs={{0,64},{64,0},{32,96},{96,32},{1,65},{65,1},{33,97},{97,33},{2,66}... | collective-permute-start | bytes 294920 | tf_op jit(solution)/shard_map/ppermute | solution.py:22
  152.7 43.6 %collective-permute-start.2 = (bf16[96,512]{1,0:T(8,128)(2,1)S(1)}, bf16[96,512]{1,0:T(8,128)(2,1)S(1)}, u32[]{:S(2)}, u32[]{:S(2)}) collective-permute-start(bf16[96,512]{1,0:T(8,128)(2,1)S(1)} %get-tuple-element.39), channel_id=1, source_target_pairs={{0,64},{64,0},{32,96},{96,32},{1,65},{65,1},{33,97},{97,33},{2,66}... | collective-permute-start | bytes 294920 | tf_op jit(solution)/shard_map/ppermute | solution.py:22
  153.4 45.0 %collective-permute-start.3 = (bf16[96,512]{1,0:T(8,128)(2,1)S(1)}, bf16[96,512]{1,0:T(8,128)(2,1)S(1)}, u32[]{:S(2)}, u32[]{:S(2)}) collective-permute-start(bf16[96,512]{1,0:T(8,128)(2,1)S(1)} %get-tuple-element.40), channel_id=1, source_target_pairs={{0,64},{64,0},{32,96},{96,32},{1,65},{65,1},{33,97},{97,33},{2,66}... | collective-permute-start | bytes 294920 | tf_op jit(solution)/shard_map/ppermute | solution.py:22
  154.7 45.8 %collective-permute-start.4 = (bf16[96,512]{1,0:T(8,128)(2,1)S(1)}, bf16[96,512]{1,0:T(8,128)(2,1)S(1)}, u32[]{:S(2)}, u32[]{:S(2)}) collective-permute-start(bf16[96,512]{1,0:T(8,128)(2,1)S(1)} %get-tuple-element.41), channel_id=1, source_target_pairs={{0,64},{64,0},{32,96},{96,32},{1,65},{65,1},{33,97},{97,33},{2,66}... | collective-permute-start | bytes 294920 | tf_op jit(solution)/shard_map/ppermute | solution.py:22
  185.2 17.1 %collective-permute-start.5 = (bf16[96,512]{1,0:T(8,128)(2,1)S(1)}, bf16[96,512]{1,0:T(8,128)(2,1)S(1)}, u32[]{:S(2)}, u32[]{:S(2)}) collective-permute-start(bf16[96,512]{1,0:T(8,128)(2,1)S(1)} %get-tuple-element.42), channel_id=1, source_target_pairs={{0,64},{64,0},{32,96},{96,32},{1,65},{65,1},{33,97},{97,33},{2,66}... | collective-permute-start | bytes 294920 | tf_op jit(solution)/shard_map/ppermute | solution.py:22
  202.9 5.9 %collective-permute-start.7 = (bf16[192,256]{1,0:T(8,128)(2,1)S(1)}, bf16[192,256]{1,0:T(8,128)(2,1)S(1)}, u32[]{:S(2)}, u32[]{:S(2)}) collective-permute-start(bf16[192,256]{1,0:T(8,128)(2,1)S(1)} %get-tuple-element.45), channel_id=1, source_target_pairs={{0,64},{64,0},{32,96},{96,32},{1,65},{65,1},{33,97},{97,33},{2,66}... | collective-permute-start | bytes 294920 | tf_op jit(solution)/shard_map/ppermute | solution.py:22
  205.4 7.0 %collective-permute-start.9 = (bf16[192,256]{1,0:T(8,128)(2,1)S(1)}, bf16[192,256]{1,0:T(8,128)(2,1)S(1)}, u32[]{:S(2)}, u32[]{:S(2)}) collective-permute-start(bf16[192,256]{1,0:T(8,128)(2,1)S(1)} %get-tuple-element.43), channel_id=1, source_target_pairs={{0,64},{64,0},{32,96},{96,32},{1,65},{65,1},{33,97},{97,33},{2,66}... | collective-permute-start | bytes 294920 | tf_op jit(solution)/shard_map/ppermute | solution.py:22
  205.5 6.9 %collective-permute-start.8 = (bf16[192,256]{1,0:T(8,128)(2,1)S(1)}, bf16[192,256]{1,0:T(8,128)(2,1)S(1)}, u32[]{:S(2)}, u32[]{:S(2)}) collective-permute-start(bf16[192,256]{1,0:T(8,128)(2,1)S(1)} %get-tuple-element.44), channel_id=1, source_target_pairs={{0,64},{64,0},{32,96},{96,32},{1,65},{65,1},{33,97},{97,33},{2,66}... | collective-permute-start | bytes 294920 | tf_op jit(solution)/shard_map/ppermute | solution.py:22
  212.5 2.3 collective-permute-start.10
  265.5 0.8 copy-start.1

commit v4 on v3

--- a/solution.py
+++ b/solution.py
@@ -280,6 +280,49 @@
     )(core, arrived)
 
 
+def own_down_kernel(core_ref, act_ref, down_ref, out_ref, weights, sems):
+    parts, size, half = weights.shape
+    columns = pl.ds(pl.multiple_of(core_ref[0] * half, half), half)
+    copies = [
+        pltpu.make_async_copy(down_ref.at[pl.ds(i * size, size), columns], weights.at[i], sems.at[i])
+        for i in range(parts)
+    ]
+    for copy in copies:
+        copy.start()
+    for i, copy in enumerate(copies):
+        copy.wait()
+        out_ref[:, i * size : (i + 1) * size] = lax.dot_general(
+            act_ref[...], weights[i], (((1,), (1,)), ((), ())), preferred_element_type=jnp.float32
+        )
+
+
+def own_down(core, act, down):
+    slots, half = act.shape
+    share = down.shape[0]
+    parts = 2
+    return pl.pallas_call(
+        own_down_kernel,
+        in_specs=[
+            pl.BlockSpec(memory_space=pltpu.SMEM),
+            pl.BlockSpec(memory_space=pltpu.VMEM),
+            pl.BlockSpec(memory_space=pltpu.HBM),
+        ],
+        out_specs=pl.BlockSpec(memory_space=pltpu.VMEM),
+        out_shape=jax.ShapeDtypeStruct((slots, share), jnp.float32),
+        scratch_shapes=[
+            pltpu.VMEM((parts, share // parts, half), down.dtype),
+            pltpu.SemaphoreType.DMA((parts,)),
+        ],
+        compiler_params=pltpu.CompilerParams(vmem_limit_bytes=24 << 20),
+        cost_estimate=pl.CostEstimate(
+            flops=2 * slots * share * half,
+            bytes_accessed=2 * half * share + 4 * slots * share,
+            transcendentals=0,
+        ),
+        name="own_down",
+    )(core, act, down)
+
+
 def layer(tokens, route_ids, gate_values, cap_limit, update_ids, expert_weights):
     steps, rows, width = tokens.shape
     experts, _, _ = expert_weights.shape
@@ -297,9 +340,8 @@
     )
     core = (fsdp_at % 2).astype(jnp.int32)
     upper = fsdp_at // 2 == 1
-    second = core == 1
-    outgoing, down_raw, combine, core, upper, second = lax.optimization_barrier(
-        (outgoing, down_raw, combine, core, upper, second)
+    outgoing, down_raw, combine, core, upper = lax.optimization_barrier(
+        (outgoing, down_raw, combine, core, upper)
     )
     arrived = exchange(outgoing)
     arrived, down_raw = lax.optimization_barrier((arrived, down_raw))
@@ -316,10 +358,12 @@
     other = swap_rows(act, 3)
     act = jnp.concatenate([jnp.where(upper, other, act), jnp.where(upper, act, other)], axis=1)
     other = lax.ppermute(act, "fsdp", CORE_SWAP)
-    act = jnp.concatenate([jnp.where(second, other, act), jnp.where(second, act, other)], axis=1)
-    out = lax.dot_general(
-        act, down, (((1,), (1,)), ((), ())), preferred_element_type=jnp.float32
-    ).astype(jnp.bfloat16)
+    own_part = own_down(core.reshape(1), act, down)
+    other_down = lax.dynamic_slice_in_dim(down, (1 - core) * half, half, axis=1)
+    out = own_part + lax.dot_general(
+        other, other_down, (((1,), (1,)), ((), ())), preferred_element_type=jnp.float32
+    )
+    out = out.astype(jnp.bfloat16)
     rest = out[main:].reshape(experts, 14, 256)
     rest = jnp.pad(rest, ((0, 0), (0, 2), (0, 0)))
     going = jnp.concatenate([out[:main].reshape(experts, 16, share), rest], axis=2)

time: 268 us -> 268 us (level)
  Pallas kernels: 20.9 us -> 23.7 us
    pallas_call x0 -> x1, Pallas kernels: none -> 2.81 us  [own_down(): pl.pallas_call(own_down_kernel, in_specs=[pl.BlockSpec(memory_space=pltpu...]
  transfers between devices with their start and end apart: 12 -> 12, of which waited for: 8 -> 9; matrix products, arithmetic and copies ran while one was open for 1% -> 1% of each run, Pallas kernels for 0% -> 1%
where the time goes in v4:
time: 268 us
  blocking collectives  168 us (63%)
  waiting for transfers between devices  47.5 us (18%)
  Pallas kernels  23.7 us (9%)
  starting transfers between devices  18.9 us (7%)
  matrix products  4.05 us (2%)
  other arithmetic  3.7 us (1%)
    all_to_all x2, blocking collectives, exchange(): lax.all_to_all(block, 'expert', split_axis=0, concat_axis=0, tiled=True)  168 us
    ppermute x9, waiting for transfers between devices, swap_rows(): lax.ppermute(block[i * size:(i + 1) * size], 'fsdp', CHIP_SWAP)  47.5 us
    ppermute x9, starting transfers between devices, swap_rows(): lax.ppermute(block[i * size:(i + 1) * size], 'fsdp', CHIP_SWAP)  13.6 us
    pallas_call x1, Pallas kernels, pack(): pl.pallas_call(functools.partial(pack_kernel, steps, rows, top, slot_coun...  11.6 us
    pallas_call x1, Pallas kernels, gate_up(): pl.pallas_call(gate_up_kernel, in_specs=[pl.BlockSpec(memory_space=pltpu....  9.27 us
  transfers between devices with their start and end apart: 12, of which 9 were waited for; matrix products, arithmetic and copies ran while one was open for 1% of the time, Pallas kernels for 1%

profile of v4, /device:TPU:0, one launch (start us, length us, event | category | flops | bytes accessed | tf_op | source)
XLA Modules:
  0.0 267.7 jit_solution(2449585979092456938)
XLA Ops:
  0.0 11.6 %pack.1 = (bf16[32,56,2688]{2,1,0:T(8,128)(2,1)}, bf16[32,56,1024]{2,1,0:T(8,128)(2,1)}, bf16[48,576]{1,0:T(8,128)(2,1)}) custom-call(s32[1]{0:T(128)} %bitcast.at_ref, s32[24,16]{1,0:T(8,128)} %bitcast.21, bf16[24,16]{1,0:T(8,128)(2,1)} %bitcast.22, s32[1,32]{1,0:T(1,128)} %bitcast.23, s32[1,32]{1,0:T(1,128)} %bitcast.24, bf16[48,7168]{1,0:T(8,128)(2,1)} %bitcast.20, ...), custom_call_target="tpu_custom_call" | custom-call | tf_op jit(solution)/shard_map/pack/pallas_call | solution.py:176
  11.6 122.3 %all_to_all.15.arrived_ref = bf16[32,56,2688]{2,1,0:T(8,128)(2,1)} all-to-all(bf16[32,56,2688]{2,1,0:T(8,128)(2,1)} %get-tuple-element.23), channel_id=1, replica_groups=mesh['fsdp'=4,'expert'=32] {'expert'}, dimensions={0} | all-to-all | bytes 19267584 | tf_op jit(solution)/shard_map/all_to_all | solution.py:16
  133.9 9.3 %gate_up.1 = (f32[576,1024]{1,0:T(8,128)}, f32[576,1024]{1,0:T(8,128)}) custom-call(s32[1]{0:T(128)} %bitcast.8.core_ref, bf16[32,56,2688]{2,1,0:T(8,128)(2,1)} %all_to_all.15.arrived_ref), custom_call_target="tpu_custom_call" | custom-call | flops 4227858432 | bytes 14352384 | tf_op jit(solution)/shard_map/gate_up/pallas_call | solution.py:259
  143.2 0.0 copy-start
  143.2 0.1 collective-permute-start
  143.3 5.0 %all-to-all-start.1 = ((bf16[32,56,1024]{2,1,0:T(8,128)(2,1)}), bf16[32,56,1024]{2,1,0:T(8,128)(2,1)}, u32[]{:S(2)}, u32[]{:S(2)}) async-start(bf16[32,56,1024]{2,1,0:T(8,128)(2,1)} %get-tuple-element.28), calls=%async_computation.1 | async-start | bytes 7340032 | tf_op jit(solution)/shard_map/all_to_all | solution.py:16
  148.3 0.0 collective-permute-done
  148.3 0.0 copy-done
  148.3 2.1 add.30
  150.4 0.1 select_convert_fusion
  150.6 0.8 collective-permute-start.1
  151.3 1.3 collective-permute-start.2
  152.7 0.7 collective-permute-start.3
  153.4 1.3 collective-permute-start.4
  154.7 0.7 collective-permute-start.5
  155.4 29.8 %collective-permute-done.1 = bf16[96,512]{1,0:T(8,128)(2,1)S(1)} collective-permute-done((bf16[96,512]{1,0:T(8,128)(2,1)S(1)}, bf16[96,512]{1,0:T(8,128)(2,1)S(1)}, u32[]{:S(2)}, u32[]{:S(2)}) %collective-permute-start.1) | collective-permute-done | bytes 98336 | tf_op jit(solution)/shard_map/ppermute | solution.py:22
  185.2 4.2 %collective-permute-start.6 = (bf16[96,512]{1,0:T(8,128)(2,1)S(1)}, bf16[96,512]{1,0:T(8,128)(2,1)S(1)}, u32[]{:S(2)}, u32[]{:S(2)}) collective-permute-start(bf16[96,512]{1,0:T(8,128)(2,1)S(1)} %get-tuple-element.33), channel_id=1, source_target_pairs={{0,64},{64,0},{32,96},{96,32},{1,65},{65,1},{33,97},{97,33},{2,66}... | collective-permute-start | bytes 294920 | tf_op jit(solution)/shard_map/ppermute | solution.py:22
  189.4 4.6 %collective-permute-done.2 = bf16[96,512]{1,0:T(8,128)(2,1)S(1)} collective-permute-done((bf16[96,512]{1,0:T(8,128)(2,1)S(1)}, bf16[96,512]{1,0:T(8,128)(2,1)S(1)}, u32[]{:S(2)}, u32[]{:S(2)}) %collective-permute-start.2) | collective-permute-done | bytes 98336 | tf_op jit(solution)/shard_map/ppermute | solution.py:22
  194.1 2.2 collective-permute-done.3
  196.3 2.1 collective-permute-done.4
  198.4 2.1 collective-permute-done.5
  200.5 1.8 collective-permute-done.6
  202.3 0.1 convert_element_type.15
  202.4 0.4 fusion.6
  202.8 2.6 collective-permute-start.7
  205.4 0.1 collective-permute-start.8
  205.5 1.9 collective-permute-start.9
  207.4 1.4 collective-permute-done.7
  208.8 2.3 collective-permute-done.8
  211.1 1.3 collective-permute-done.9
  212.5 0.3 collective-permute-start.10
  212.7 0.0 all-to-all-done.1
  212.8 2.8 %own_down.1 = f32[576,1792]{1,0:T(8,128)S(1)} custom-call(s32[1]{0:T(128)} %bitcast.8.core_ref, bf16[576,512]{1,0:T(8,128)(2,1)S(1)} %pad_maximum_fusion.act_ref, bf16[1792,1024]{1,0:T(8,128)(2,1)} %bitcast.9.down_ref), custom_call_target="tpu_custom_call" | custom-call | flops 1056964608 | bytes 5963776 | tf_op jit(solution)/shard_map/own_down/pallas_call | solution.py:303
  215.6 0.0 collective-permute-done.10
  215.6 2.8 %fusion.3 = f32[576,1792]{1,0:T(8,128)S(1)} fusion(bf16[576,512]{1,0:T(8,128)(2,1)S(1)} %collective-permute-done.10, bf16[1792,1024]{1,0:T(8,128)(2,1)} %bitcast.9.down_ref, s32[]{:T(128)S(6)} %select_n.53), kind=kOutput, calls=%fused_computation.6 | convolution fusion | flops 1056964608 | bytes 6553604 | tf_op jit(solution)/shard_map/dot_general | solution.py:363
  218.4 0.6 add_convert_fusion
  219.0 0.1 slice.103
  219.1 0.3 reshape.49
  219.3 0.3 fusion.2
  219.6 45.9 %all_to_all.16 = bf16[32,16,2048]{2,1,0:T(8,128)(2,1)S(1)} all-to-all(bf16[32,16,2048]{2,1,0:T(8,128)(2,1)S(1)} %fusion.2), channel_id=1, replica_groups=mesh['fsdp'=4,'expert'=32] {'expert'}, dimensions={0} | all-to-all | bytes 4194304 | tf_op jit(solution)/shard_map/all_to_all | solution.py:16
  265.5 0.0 copy-start.1
  265.6 0.3 reshape.51
  265.8 0.2 slice.105
  266.0 0.4 copy-done.1
  266.4 0.4 fusion.12
  266.8 0.9 fusion.1
  (15 shorter events, 0.3 us)
Async XLA Ops:
  143.2 5.1 %copy-start = (f32[576,1024]{1,0:T(8,128)S(1)}, f32[576,1024]{1,0:T(8,128)}, u32[]{:S(2)}) copy-start(f32[576,1024]{1,0:T(8,128)} %get-tuple-element.26) | copy-start | bytes 7077892
  143.2 5.1 %collective-permute-start = (f32[576,1024]{1,0:T(8,128)}, f32[576,1024]{1,0:T(8,128)}, u32[]{:S(2)}, u32[]{:S(2)}) collective-permute-start(f32[576,1024]{1,0:T(8,128)} %get-tuple-element.27), channel_id=1, source_target_pairs={{0,32},{32,0},{64,96},{96,64},{1,33},{33,1},{65,97},{97,65},{2,34}... | collective-permute-start | bytes 7077896 | tf_op jit(solution)/shard_map/ppermute | solution.py:351
  143.3 69.5 %all-to-all-start.1 = ((bf16[32,56,1024]{2,1,0:T(8,128)(2,1)}), bf16[32,56,1024]{2,1,0:T(8,128)(2,1)}, u32[]{:S(2)}, u32[]{:S(2)}) async-start(bf16[32,56,1024]{2,1,0:T(8,128)(2,1)} %get-tuple-element.28), calls=%async_computation.1 | async-start | bytes 7340032 | tf_op jit(solution)/shard_map/all_to_all | solution.py:16
  150.6 34.6 %collective-permute-start.1 = (bf16[96,512]{1,0:T(8,128)(2,1)S(1)}, bf16[96,512]{1,0:T(8,128)(2,1)S(1)}, u32[]{:S(2)}, u32[]{:S(2)}) collective-permute-start(bf16[96,512]{1,0:T(8,128)(2,1)S(1)} %get-tuple-element.34), channel_id=1, source_target_pairs={{0,64},{64,0},{32,96},{96,32},{1,65},{65,1},{33,97},{97,33},{2,66}... | collective-permute-start | bytes 294920 | tf_op jit(solution)/shard_map/ppermute | solution.py:22
  151.3 42.7 %collective-permute-start.2 = (bf16[96,512]{1,0:T(8,128)(2,1)S(1)}, bf16[96,512]{1,0:T(8,128)(2,1)S(1)}, u32[]{:S(2)}, u32[]{:S(2)}) collective-permute-start(bf16[96,512]{1,0:T(8,128)(2,1)S(1)} %get-tuple-element.35), channel_id=1, source_target_pairs={{0,64},{64,0},{32,96},{96,32},{1,65},{65,1},{33,97},{97,33},{2,66}... | collective-permute-start | bytes 294920 | tf_op jit(solution)/shard_map/ppermute | solution.py:22
  152.7 43.6 %collective-permute-start.3 = (bf16[96,512]{1,0:T(8,128)(2,1)S(1)}, bf16[96,512]{1,0:T(8,128)(2,1)S(1)}, u32[]{:S(2)}, u32[]{:S(2)}) collective-permute-start(bf16[96,512]{1,0:T(8,128)(2,1)S(1)} %get-tuple-element.36), channel_id=1, source_target_pairs={{0,64},{64,0},{32,96},{96,32},{1,65},{65,1},{33,97},{97,33},{2,66}... | collective-permute-start | bytes 294920 | tf_op jit(solution)/shard_map/ppermute | solution.py:22
  153.4 45.0 %collective-permute-start.4 = (bf16[96,512]{1,0:T(8,128)(2,1)S(1)}, bf16[96,512]{1,0:T(8,128)(2,1)S(1)}, u32[]{:S(2)}, u32[]{:S(2)}) collective-permute-start(bf16[96,512]{1,0:T(8,128)(2,1)S(1)} %get-tuple-element.37), channel_id=1, source_target_pairs={{0,64},{64,0},{32,96},{96,32},{1,65},{65,1},{33,97},{97,33},{2,66}... | collective-permute-start | bytes 294920 | tf_op jit(solution)/shard_map/ppermute | solution.py:22
  154.7 45.8 %collective-permute-start.5 = (bf16[96,512]{1,0:T(8,128)(2,1)S(1)}, bf16[96,512]{1,0:T(8,128)(2,1)S(1)}, u32[]{:S(2)}, u32[]{:S(2)}) collective-permute-start(bf16[96,512]{1,0:T(8,128)(2,1)S(1)} %get-tuple-element.38), channel_id=1, source_target_pairs={{0,64},{64,0},{32,96},{96,32},{1,65},{65,1},{33,97},{97,33},{2,66}... | collective-permute-start | bytes 294920 | tf_op jit(solution)/shard_map/ppermute | solution.py:22
  185.2 17.1 %collective-permute-start.6 = (bf16[96,512]{1,0:T(8,128)(2,1)S(1)}, bf16[96,512]{1,0:T(8,128)(2,1)S(1)}, u32[]{:S(2)}, u32[]{:S(2)}) collective-permute-start(bf16[96,512]{1,0:T(8,128)(2,1)S(1)} %get-tuple-element.33), channel_id=1, source_target_pairs={{0,64},{64,0},{32,96},{96,32},{1,65},{65,1},{33,97},{97,33},{2,66}... | collective-permute-start | bytes 294920 | tf_op jit(solution)/shard_map/ppermute | solution.py:22
  202.8 5.9 %collective-permute-start.7 = (bf16[192,256]{1,0:T(8,128)(2,1)S(1)}, bf16[192,256]{1,0:T(8,128)(2,1)S(1)}, u32[]{:S(2)}, u32[]{:S(2)}) collective-permute-start(bf16[192,256]{1,0:T(8,128)(2,1)S(1)} %get-tuple-element.41), channel_id=1, source_target_pairs={{0,64},{64,0},{32,96},{96,32},{1,65},{65,1},{33,97},{97,33},{2,66}... | collective-permute-start | bytes 294920 | tf_op jit(solution)/shard_map/ppermute | solution.py:22
  205.4 5.7 %collective-permute-start.8 = (bf16[192,256]{1,0:T(8,128)(2,1)S(1)}, bf16[192,256]{1,0:T(8,128)(2,1)S(1)}, u32[]{:S(2)}, u32[]{:S(2)}) collective-permute-start(bf16[192,256]{1,0:T(8,128)(2,1)S(1)} %get-tuple-element.40), channel_id=1, source_target_pairs={{0,64},{64,0},{32,96},{96,32},{1,65},{65,1},{33,97},{97,33},{2,66}... | collective-permute-start | bytes 294920 | tf_op jit(solution)/shard_map/ppermute | solution.py:22
  205.5 6.9 %collective-permute-start.9 = (bf16[192,256]{1,0:T(8,128)(2,1)S(1)}, bf16[192,256]{1,0:T(8,128)(2,1)S(1)}, u32[]{:S(2)}, u32[]{:S(2)}) collective-permute-start(bf16[192,256]{1,0:T(8,128)(2,1)S(1)} %get-tuple-element.39), channel_id=1, source_target_pairs={{0,64},{64,0},{32,96},{96,32},{1,65},{65,1},{33,97},{97,33},{2,66}... | collective-permute-start | bytes 294920 | tf_op jit(solution)/shard_map/ppermute | solution.py:22
  212.5 3.1 %collective-permute-start.10 = (bf16[576,512]{1,0:T(8,128)(2,1)S(1)}, bf16[576,512]{1,0:T(8,128)(2,1)S(1)}, u32[]{:S(2)}, u32[]{:S(2)}) collective-permute-start(bf16[576,512]{1,0:T(8,128)(2,1)S(1)} %pad_maximum_fusion.act_ref), channel_id=1, source_target_pairs={{0,32},{32,0},{64,96},{96,64},{1,33},{33,1},{65,97},{97,65},{2,34}... | collective-permute-start | bytes 1769480 | tf_op jit(solution)/shard_map/ppermute | solution.py:360
  265.5 0.8 copy-start.1
